TPU v7x, 128 devices: a whole 4x4x4 slice. The times are simulated.
128 devices in a mesh: seq: 64 (over y_hi, z, x, core), dp: 2 (over y_lo).
Axes of the slice: x: 4, y: 4 (y_hi: 2, y_lo: 2; y = y_hi * 2 + y_lo), z: 4, core: 2. Of those that a mesh axis runs over, the one named last changes fastest.
Arguments:
- inputs: bfloat16 [2, 32768, 4096], P('dp', 'seq'), may hold values from -60 to 60
- cotangent: bfloat16 [2, 32768, 4096], P('dp', 'seq'), may hold values from -16 to 16
- w_qkv: bfloat16 [4096, 768], replicated, may hold values from -0.09375 to 0.09375
- w_out: bfloat16 [512, 4096], replicated, may hold values from -0.25 to 0.25
- doc_start: int32 [2, 32768], P('dp', 'seq'), may hold values from 0 to 31744, as said below
Outputs:
- input_grad: bfloat16 [2, 32768, 4096], P('dp', 'seq')
- qkv_grad: float32 [4096, 768], P(('seq', 'dp'))
- out_grad: float32 [512, 4096], P(None, ('seq', 'dp'))
Inputs may be any that keep to these rules, and one draw needn't show every extreme that they name: doc_start[b, p] is the first position of the document holding position p of row b; documents are contiguous runs. Cut a row into blocks of 512 positions: a document lies inside one block and then begins at a multiple of 64, or it fills exactly w whole blocks, w a power of two from 2 to 4, beginning at block 0 or at a block whose index minus 4/2 is a multiple of w. The first 2 blocks of a row form one document, and so do the last 2 blocks; the two blocks at the middle of a row lie in one document of 4 blocks.
All inputs are finite; a program needn't handle non-finite values.
Results may differ from a plain program's by a relative error of at most 0.025.
The roundings to bfloat16 on the way count: a program that leaves them out, or rounds other values in their place, can miss the bound.
Values may be sent and summed in bfloat16 or wider, within the bound.
A program may use at most 128 MiB of HBM per device.

v0:
```python
import jax
import jax.numpy as jnp
from jax import lax
from jax.experimental import pallas as pl
from jax.experimental.pallas import tpu as pltpu
from jax.sharding import PartitionSpec as P

HEAD = 128
HEADS = 4
SPAN = 4


rope_theta = 500000.0


def from_behind(block, axis, distance):
    devices = range(lax.axis_size(axis))
    route = [(i - distance, i) for i in devices if i - distance in devices]
    return lax.ppermute(block, axis, route)


def rope_tables(offsets):
    half_width = HEAD // 2
    frequency = rope_theta ** (-2.0 * jnp.arange(half_width, dtype=jnp.float32) / HEAD)
    angles = offsets.astype(jnp.float32)[:, None] * frequency[None, :]
    angles = jnp.concatenate([angles, angles], axis=1)
    return (jnp.cos(angles), jnp.sin(angles))


def rotate(vector, cosine_table, sine_table):
    half_width = vector.shape[-1] // 2
    rotated = jnp.concatenate([-vector[..., half_width:], vector[..., :half_width]], axis=-1)
    return vector * cosine_table + rotated * sine_table


def rotate_back(gradient, cosine_table, sine_table):
    half_width = gradient.shape[-1] // 2
    weighted = gradient * sine_table
    return gradient * cosine_table + jnp.concatenate(
        [weighted[..., half_width:], -weighted[..., :half_width]], axis=-1
    )


AXES = 4
ROWS = 32
LANES = 128
STREAMS = 10
BF16 = jnp.bfloat16
F32 = jnp.float32
MESH_ID = pl.DeviceIdType.MESH


def even_pair(i):
    return i + 1 - 2 * (i % 2)


def odd_pair(i):
    return (i + 3 - 2 * (i % 2)) % AXES


def stream_plan(g):
    order = ((0, 1, 2), (1, 2, 0), (2, 0, 1))[g % 3]
    first, second = (even_pair, odd_pair) if (g // 3) % 2 == 0 else (odd_pair, even_pair)
    return order, first, second


def device_of(x, y, z, core):
    return ((((y // 2) * AXES + z) * AXES + x) * 2 + core, y % 2)


def reduce_kernel(q_ref, o_ref, q_out, o_out, q_in, o_in, held, r1a, r1b, r2a, r2b, r3a, r3b, sib_sem, send_sem, recv_sem):
    seq = lax.axis_index("seq")
    dp = lax.axis_index("dp")
    core = seq % 2
    here = ((seq // 2) % AXES, (seq // 32) * 2 + dp, (seq // 8) % AXES)
    sibling = device_of(here[0], here[1], here[2], 1 - core)

    def moved(axis, value):
        spot = list(here)
        spot[axis] = value
        return device_of(*spot, core)

    barrier = pltpu.get_barrier_semaphore()
    pl.semaphore_signal(barrier, inc=1, device_id=sibling, device_id_type=MESH_ID)
    for axis in range(3):
        for pair in (even_pair, odd_pair):
            pl.semaphore_signal(barrier, inc=1, device_id=moved(axis, pair(here[axis])), device_id_type=MESH_ID)
    pl.semaphore_wait(barrier, 7)

    swaps = []
    for n, (src, dst) in enumerate(((q_ref, q_in), (o_ref, o_in))):
        swap = pltpu.make_async_remote_copy(
            src_ref=src.at[:, 1 - core],
            dst_ref=dst,
            send_sem=sib_sem.at[0, n],
            recv_sem=sib_sem.at[1, n],
            device_id=sibling,
            device_id_type=MESH_ID,
        )
        swap.start()
        swaps.append(swap)
    for swap in swaps:
        swap.wait_recv()

    def combine(block, _):
        y_hi = block // 16
        z = (block // 4) % 4
        x = block % 4
        for y_lo in range(2):
            spot = (x, y_hi * 2 + y_lo, z)
            rows = slice(y_lo * ROWS, (y_lo + 1) * ROWS)
            for g in range(STREAMS):
                order, _, _ = stream_plan(g)
                place = (spot[order[0]] * AXES + spot[order[1]]) * AXES + spot[order[2]]
                src, got, col = (q_ref, q_in, g) if g < 6 else (o_ref, o_in, g - 6)
                cols = slice(col * LANES, (col + 1) * LANES)
                total = src[block, core, rows, cols].astype(F32) + got[block, rows, cols].astype(F32)
                held[g, place] = total.astype(BF16)
        return 0

    lax.fori_loop(0, 32, combine, 0)

    def copy(src, dst, g, n, target):
        return pltpu.make_async_remote_copy(
            src_ref=src,
            dst_ref=dst,
            send_sem=send_sem.at[g, n],
            recv_sem=recv_sem.at[g, n],
            device_id=target,
            device_id_type=MESH_ID,
        )

    def add_into(dst, dst_at, src, src_at, count):
        def step(k, _):
            dst[dst_at + (k,)] = (dst[dst_at + (k,)].astype(F32) + src[src_at(k)].astype(F32)).astype(BF16)
            return 0

        if count == 1:
            step(0, 0)
        else:
            lax.fori_loop(0, count, step, 0)

    bufs = ((r1a, r1b), (r2a, r2b), (r3a, r3b))
    sizes = (16, 4, 1)
    sends = {}

    def source(g, stage):
        if stage == 0:
            return held, g
        return bufs[stage - 1][1], g

    def start_first(g, stage):
        order, first, second = stream_plan(g)
        i = here[order[stage]]
        size = sizes[stage]
        f = first(i)
        src, _ = source(g, stage)
        for slot, index in ((1, second(f)), (0, f)):
            sends[g, stage, slot] = copy(
                src.at[g, pl.ds(index * size, size)],
                bufs[stage][0].at[g, slot],
                g,
                stage * 3 + slot,
                moved(order[stage], f),
            )
            sends[g, stage, slot].start()

    for g in range(STREAMS):
        start_first(g, 0)
    for stage in range(3):
        size = sizes[stage]
        for g in range(STREAMS):
            order, first, second = stream_plan(g)
            i = here[order[stage]]
            s = second(i)
            src, _ = source(g, stage)
            sends[g, stage, 1].wait_recv()
            add_into(bufs[stage][0], (g, 1), src, lambda k, s=s, g=g: (g, s * size + k), size)
            sends[g, stage, 2] = copy(bufs[stage][0].at[g, 1], bufs[stage][1].at[g], g, stage * 3 + 2, moved(order[stage], s))
            sends[g, stage, 2].start()
            sends[g, stage, 0].wait_recv()
            add_into(bufs[stage][0], (g, 0), src, lambda k, i=i, g=g: (g, i * size + k), size)
        for g in range(STREAMS):
            sends[g, stage, 2].wait_recv()
            if stage < 2:
                add_into(bufs[stage][1], (g,), bufs[stage][0], lambda k, g=g: (g, 0, k), size)
                start_first(g, stage + 1)
            else:
                total = r3b[g, 0].astype(F32) + r3a[g, 0, 0].astype(F32)
                if g < 6:
                    q_out[:, g * LANES : (g + 1) * LANES] = total
                else:
                    o_out[:, (g - 6) * LANES : (g - 5) * LANES] = total
    for swap in swaps:
        swap.wait_send()
    for send in sends.values():
        send.wait_send()


def reduce_terms(q_term, o_term):
    vmem = pl.BlockSpec(memory_space=pltpu.VMEM)
    tile = (ROWS, LANES)
    return pl.pallas_call(
        reduce_kernel,
        out_shape=(
            jax.ShapeDtypeStruct((ROWS, 768), F32),
            jax.ShapeDtypeStruct((ROWS, 512), F32),
        ),
        in_specs=[vmem, vmem],
        out_specs=(vmem, vmem),
        scratch_shapes=[
            pltpu.VMEM((32, 2 * ROWS, 768), BF16),
            pltpu.VMEM((32, 2 * ROWS, 512), BF16),
            pltpu.VMEM((STREAMS, 64) + tile, BF16),
            pltpu.VMEM((STREAMS, 2, 16) + tile, BF16),
            pltpu.VMEM((STREAMS, 16) + tile, BF16),
            pltpu.VMEM((STREAMS, 2, 4) + tile, BF16),
            pltpu.VMEM((STREAMS, 4) + tile, BF16),
            pltpu.VMEM((STREAMS, 2, 1) + tile, BF16),
            pltpu.VMEM((STREAMS, 1) + tile, BF16),
            pltpu.SemaphoreType.DMA((2, 2)),
            pltpu.SemaphoreType.DMA((STREAMS, 9)),
            pltpu.SemaphoreType.DMA((STREAMS, 9)),
        ],
        compiler_params=pltpu.CompilerParams(
            collective_id=0, has_side_effects=True, vmem_limit_bytes=60 * 1024 * 1024
        ),
    )(q_term.reshape(32, 2, 2 * ROWS, 768), o_term.reshape(32, 2, 2 * ROWS, 512))


NT = (((1,), (1,)), ((), ()))
NN = (((1,), (0,)), ((), ()))
TN = (((0,), (0,)), ((), ()))
LOG2E = 1.4426950408889634
TOK = 512
QROWS = 256
FAR = -1e30


def mm(a, b, dims):
    return lax.dot_general(a, b, dims, preferred_element_type=F32)


def attention_kernel(first_ref, q_ref, g_ref, kv_ref, start_ref, att_ref, dq_ref, dkv_ref):
    scale = HEAD**-0.5
    c = scale * LOG2E
    dkv_ref[...] = jnp.zeros_like(dkv_ref)
    first = first_ref[0]

    def head(h, _):
        cols = pl.ds(pl.multiple_of(h * HEAD, HEAD), HEAD)
        for block in range(TOK // QROWS):
            rows = slice(block * QROWS, (block + 1) * QROWS)
            q = q_ref[rows, cols]
            g = g_ref[rows, cols]
            start = start_ref[rows, :]
            widths = [(block + 1) * QROWS] + [TOK] * (SPAN - 1)
            scores, bias = [], []
            top = None
            for d in range(SPAN):
                s = mm(q, kv_ref[d, : widths[d], :HEAD], NT)
                if d == 0:
                    col = lax.broadcasted_iota(jnp.int32, s.shape, 1)
                    row = lax.broadcasted_iota(jnp.int32, s.shape, 0) + block * QROWS
                    s = jnp.where((col <= row) & (col >= start - first), s, FAR)
                    b = 0.0
                    top = jnp.max(s, axis=1, keepdims=True)
                else:
                    b = jnp.where(start <= first - d * TOK, 0.0, FAR)
                    top = jnp.maximum(top, jnp.max(s, axis=1, keepdims=True) + b)
                scores.append(s)
                bias.append(b)
            top = top * c
            exps = [jnp.exp2(scores[d] * c + (bias[d] - top)) for d in range(SPAN)]
            inverse = 1.0 / sum(jnp.sum(e, axis=1, keepdims=True) for e in exps)
            probs = [e * inverse for e in exps]
            rounded = [p.astype(BF16) for p in probs]
            att = sum(mm(rounded[d], kv_ref[d, : widths[d], HEAD:], NN) for d in range(SPAN)).astype(BF16)
            att_ref[rows, cols] = att
            delta = jnp.sum(g.astype(F32) * att.astype(F32), axis=1, keepdims=True)
            dq = 0.0
            for d in range(SPAN):
                w = widths[d]
                dp = mm(g, kv_ref[d, :w, HEAD:], NT)
                ds = (probs[d] * (dp - delta)).astype(BF16)
                dq = dq + mm(ds, kv_ref[d, :w, :HEAD], NN)
                dkv_ref[d, :w, :HEAD] += mm(ds, q, TN)
                dkv_ref[d, :w, HEAD:] += mm(rounded[d], g, TN)
            dq_ref[rows, cols] = dq * scale
        return 0

    lax.fori_loop(0, HEADS, head, 0)
    for d in range(SPAN):
        dkv_ref[d, :, :HEAD] = dkv_ref[d, :, :HEAD] * scale


def attention(first, q, g, kv, start):
    vmem = pl.BlockSpec(memory_space=pltpu.VMEM)
    return pl.pallas_call(
        attention_kernel,
        out_shape=(
            jax.ShapeDtypeStruct((TOK, HEADS * HEAD), BF16),
            jax.ShapeDtypeStruct((TOK, HEADS * HEAD), F32),
            jax.ShapeDtypeStruct((SPAN, TOK, 2 * HEAD), F32),
        ),
        in_specs=[pl.BlockSpec(memory_space=pltpu.SMEM)] + [vmem] * 4,
        out_specs=(vmem, vmem, vmem),
        compiler_params=pltpu.CompilerParams(vmem_limit_bytes=48 * 1024 * 1024),
    )(first, q, g, kv, start)


def per_device(inputs, cotangent, w_qkv, w_out, doc_start):
    tokens = inputs[0]
    upstream = cotangent[0]
    query_start = doc_start[0]
    rows_here = tokens.shape[0]
    scaling = HEAD ** (-0.5)
    query_width = HEADS * HEAD
    device_index = lax.axis_index("seq")
    query_pos = device_index * rows_here + jnp.arange(rows_here, dtype=jnp.int32)
    cosine_table, sine_table = rope_tables(query_pos - query_start)
    projected = jnp.dot(tokens, w_qkv, preferred_element_type=jnp.float32)
    queries = rotate(
        projected[:, :query_width].reshape(rows_here, HEADS, HEAD),
        cosine_table[:, None, :],
        sine_table[:, None, :],
    ).astype(jnp.bfloat16)
    rotated_keys = rotate(projected[:, query_width : query_width + HEAD], cosine_table, sine_table)
    key_value = jnp.concatenate([rotated_keys, projected[:, query_width + HEAD :]], axis=1).astype(
        jnp.bfloat16
    )
    attended_grad = (
        lax.dot_general(
            upstream, w_out, (((1,), (1,)), ((), ())), preferred_element_type=jnp.float32
        )
        .astype(jnp.bfloat16)
        .reshape(rows_here, HEADS, HEAD)
    )
    received = [key_value]
    travelling = key_value
    for offset in range(1, SPAN):
        travelling = from_behind(travelling, "seq", 1)
        received.append(travelling)
    attended, query_grad, kv_terms = attention(
        (device_index * rows_here).reshape(1),
        queries.reshape(rows_here, query_width),
        attended_grad.reshape(rows_here, query_width),
        jnp.stack(received),
        query_start.reshape(rows_here, 1),
    )
    query_grad = query_grad.reshape(rows_here, HEADS, HEAD)
    kv_total = kv_terms[SPAN - 1]
    for offset in range(SPAN - 2, -1, -1):
        kv_total = (
            from_behind(kv_total.astype(jnp.bfloat16), "seq", -1).astype(kv_total.dtype)
            + kv_terms[offset]
        )
    query_pre = rotate_back(query_grad, cosine_table[:, None, :], sine_table[:, None, :]).reshape(
        rows_here, query_width
    )
    key_pre = rotate_back(kv_total[:, :HEAD], cosine_table, sine_table)
    merged_grad = jnp.concatenate([query_pre, key_pre, kv_total[:, HEAD:]], axis=1).astype(
        jnp.bfloat16
    )
    input_grad = lax.dot_general(
        merged_grad, w_qkv, (((1,), (1,)), ((), ())), preferred_element_type=jnp.float32
    ).astype(jnp.bfloat16)[None]
    flat_attended = attended.reshape(rows_here, query_width)
    out_term = lax.dot_general(
        upstream, flat_attended, (((0,), (0,)), ((), ())), preferred_element_type=jnp.float32
    ).astype(jnp.bfloat16)
    qkv_term = lax.dot_general(
        tokens, merged_grad, (((0,), (0,)), ((), ())), preferred_element_type=jnp.float32
    ).astype(jnp.bfloat16)
    qkv_grad, out_rows = reduce_terms(qkv_term, out_term)
    out_grad = out_rows.T
    return (input_grad, qkv_grad, out_grad)


def solution(mesh):
    return jax.shard_map(
        per_device,
        mesh=mesh,
        in_specs=(P("dp", "seq", None), P("dp", "seq", None), P(), P(), P("dp", "seq")),
        out_specs=(P("dp", "seq", None), P(("seq", "dp"), None), P(None, ("seq", "dp"))),
        check_vma=False,
    )
```

profile of v0, /device:TPU:0, one launch (start us, length us, event | category | flops | bytes accessed | tf_op | source)
XLA Modules:
  0.0 192.1 jit_solution(5006949118377770266)
XLA Ops:
  0.7 7.0 %fusion.7 = f32[512,768]{1,0:T(8,128)S(1)} fusion(bf16[4096,768]{1,0:T(8,128)(2,1)} %param.7, bf16[1,512,4096]{2,1,0:T(8,128)(2,1)} %param.5), kind=kOutput, calls=%fused_computation.10 | convolution fusion | flops 3221225472 | bytes 12058624 | tf_op jit(solution)/shard_map/dot_general | solution.py:322
  7.8 0.2 slice_negate_fusion.3
  8.0 1.8 fusion.18
  9.8 0.8 pad_maximum_fusion.6
  10.6 2.0 %collective-permute-start = (bf16[512,256]{1,0:T(8,128)(2,1)}, bf16[512,256]{1,0:T(8,128)(2,1)}, u32[]{:S(2)}, u32[]{:S(2)}) collective-permute-start(bf16[512,256]{1,0:T(8,128)(2,1)} %pad_maximum_fusion.6), channel_id=1, source_target_pairs={{0,2},{2,4},{4,6},{6,8},{8,10},{10,12},{12,14},{14,16},{16,18},{18... | collective-permute-start | bytes 786440 | tf_op jit(solution)/shard_map/ppermute | solution.py:19
  12.6 5.8 %fusion.9.g_ref = bf16[512,512]{1,0:T(8,128)(2,1)S(1)} fusion(bf16[512,4096]{1,0:T(8,128)(2,1)} %param.8, bf16[1,512,4096]{2,1,0:T(8,128)(2,1)} %param.6), kind=kOutput, calls=%fused_computation.12 | convolution fusion | flops 2147745792 | bytes 8912896 | tf_op jit(solution)/shard_map/dot_general | solution.py:333
  18.4 0.1 slice.72
  18.6 0.4 reshape.127
  19.0 3.7 %collective-permute-start.1 = (bf16[512,256]{1,0:T(8,128)(2,1)}, bf16[512,256]{1,0:T(8,128)(2,1)S(1)}, u32[]{:S(2)}, u32[]{:S(2)}) collective-permute-start(bf16[512,256]{1,0:T(8,128)(2,1)} %collective-permute-done), channel_id=1, source_target_pairs={{0,2},{2,4},{4,6},{6,8},{8,10},{10,12},{12,14},{14,16},{16,18},{18... | collective-permute-start | bytes 786440 | tf_op jit(solution)/shard_map/ppermute | solution.py:19
  22.7 0.6 slice_negate_fusion.1
  23.3 0.7 maximum_multiply_fusion
  23.9 0.1 collective-permute-done.1
  24.0 4.4 %collective-permute-start.2 = (bf16[512,256]{1,0:T(8,128)(2,1)S(1)}, bf16[512,256]{1,0:T(8,128)(2,1)S(1)}, u32[]{:S(2)}, u32[]{:S(2)}) collective-permute-start(bf16[512,256]{1,0:T(8,128)(2,1)S(1)} %collective-permute-done.1), channel_id=1, source_target_pairs={{0,2},{2,4},{4,6},{6,8},{8,10},{10,12},{12,14},{14,16},{16,18},{18... | collective-permute-start | bytes 786440 | tf_op jit(solution)/shard_map/ppermute | solution.py:19
  28.4 0.2 mul.77
  28.6 0.3 fusion.13.q_ref
  28.9 0.6 copy-done.3
  29.6 0.1 copy.10.start_ref
  29.7 1.0 slice_bitcast_fusion
  30.7 1.0 pad_maximum_fusion.kv_ref
  31.7 22.5 %shard_map.76 = (bf16[512,512]{1,0:T(8,128)(2,1)S(1)}, f32[512,512]{1,0:T(8,128)S(1)}, f32[4,512,256]{2,1,0:T(8,128)S(1)}) custom-call(s32[1]{0:T(128)} %bitcast.first_ref, bf16[512,512]{1,0:T(8,128)(2,1)S(1)} %fusion.13.q_ref, bf16[512,512]{1,0:T(8,128)(2,1)S(1)} %fusion.9.g_ref, bf16[4,512,256]{2,1,0:T(8,128)(2,1)S(1)} %pad_maximum_fusion.kv_ref, ...), custom_call_target="tpu_custom_call" | custom-call | tf_op jit(solution)/shard_map/pallas_call | solution.py:299
  54.3 1.3 copy-done
  55.6 0.8 copy-done.2
  56.4 1.3 reshape.128
  57.7 1.1 fusion.16
  58.8 1.3 collective-permute-start.3
  60.1 6.9 %fusion.1 = bf16[4096,512]{0,1:T(8,128)(2,1)} fusion(bf16[512,512]{1,0:T(8,128)(2,1)} %copy-done.2, bf16[1,512,4096]{2,1,0:T(8,128)(2,1)} %param.6), kind=kOutput, calls=%fused_computation.4 | convolution fusion | flops 2149580800 | bytes 8912896 | tf_op jit(solution)/shard_map/dot_general | solution.py:369
  67.0 0.3 broadcast_multiply_fusion
  67.3 0.1 fusion.15
  67.4 1.3 collective-permute-start.4
  68.7 2.1 %fusion.24 = (f32[512,4,64]{2,1,0:T(4,128)}, f32[512,4,64]{2,1,0:T(4,128)}) fusion(f32[512,4,128]{2,1,0:T(4,128)S(1)} %broadcast_multiply_fusion), kind=kLoop, calls=%fused_computation.53 | loop fusion | flops 131072 | bytes 2097152 | tf_op jit(solution)/shard_map/slice | solution.py:40
  70.8 6.4 %copy.12 = bf16[4096,512]{1,0:T(8,128)(2,1)} copy(bf16[4096,512]{0,1:T(8,128)(2,1)} %fusion.1) | data formatting | bytes 8388608 | tf_op jit(solution)/shard_map/convert_element_type | solution.py:371
  77.2 2.2 %pad_maximum_fusion.1 = f32[512,4,128]{2,1,0:T(4,128)S(1)} fusion(f32[512,4,64]{2,1,0:T(4,128)} %get-tuple-element.16, f32[512,4,64]{2,1,0:T(4,128)} %get-tuple-element.15), kind=kLoop, calls=%fused_computation.23 | loop fusion | flops 262144 | bytes 2097152 | tf_op jit(solution)/shard_map/concatenate | solution.py:39
  79.5 1.0 fusion.14
  80.5 1.8 collective-permute-start.5
  82.3 0.4 fusion.12
  82.7 5.4 %collective-permute-done.5 = bf16[512,256]{1,0:T(8,128)(2,1)S(1)} collective-permute-done((bf16[512,256]{1,0:T(8,128)(2,1)S(1)}, bf16[512,256]{1,0:T(8,128)(2,1)S(1)}, u32[]{:S(2)}, u32[]{:S(2)}) %collective-permute-start.5) | collective-permute-done | bytes 262176 | tf_op jit(solution)/shard_map/ppermute | solution.py:19
  88.1 0.1 bitcast_add_fusion.2
  88.2 0.9 slice_multiply_fusion.1
  89.2 0.0 slice-start
  89.2 0.1 fusion.25
  89.3 1.0 fusion.19
  90.3 0.0 slice-start.1
  90.3 5.4 %fusion = bf16[4096,768]{0,1:T(8,128)(2,1)} fusion(bf16[1,512,4096]{2,1,0:T(8,128)(2,1)S(1)} %copy-done.14, bf16[512,128]{1,0:T(8,128)(2,1)S(1)} %slice.106, bf16[512,128]{1,0:T(8,128)(2,1)S(1)} %fusion.19, bf16[512,512]{1,0:T(8,128)(2,1)S(1)} %fusion.12), kind=kOutput, calls=%fused_computation.1 | convolution fusion | flops 3226730496 | bytes 11272192 | tf_op jit(solution)/shard_map/dot_general | solution.py:372
  95.8 5.0 %fusion.2 = bf16[1,512,4096]{2,1,0:T(8,128)(2,1)} fusion(bf16[4096,768]{1,0:T(8,128)(2,1)S(1)} %bitcast.77, bf16[512,128]{1,0:T(8,128)(2,1)S(1)} %slice.106, bf16[512,128]{1,0:T(8,128)(2,1)S(1)} %fusion.19, bf16[512,512]{1,0:T(8,128)(2,1)S(1)} %fusion.12), kind=kOutput, calls=%fused_computation.5 | convolution fusion | flops 3225681920 | bytes 11272192 | tf_op jit(solution)/shard_map/dot_general | solution.py:365
  100.8 8.6 %copy.11 = bf16[4096,768]{1,0:T(8,128)(2,1)} copy(bf16[4096,768]{0,1:T(8,128)(2,1)} %fusion) | data formatting | bytes 12582912 | tf_op jit(solution)/shard_map/convert_element_type | solution.py:374
  109.4 79.6 %shard_map.77 = (f32[32,768]{1,0:T(8,128)}, f32[32,512]{1,0:T(8,128)}) custom-call(bf16[32,2,64,768]{3,2,1,0:T(8,128)(2,1)} %bitcast.64, bf16[32,2,64,512]{3,2,1,0:T(8,128)(2,1)} %bitcast.65), custom_call_target="tpu_custom_call" | custom-call | tf_op jit(solution)/shard_map/pallas_call | solution.py:203
  189.0 1.5 copy.22
  190.6 1.5 copy.23
  (38 shorter events, 0.1 us)
Async XLA Ops:
  0.7 7.1 %copy-start.13 = (s32[1,512]{1,0:T(1,128)S(1)}, s32[1,512]{1,0:T(1,128)}, u32[]{:S(2)}) copy-start(s32[1,512]{1,0:T(1,128)} %param.9) | copy-start | bytes 6148
  7.7 10.7 %copy-start.5 = (f32[512,768]{1,0:T(8,128)}, f32[512,768]{1,0:T(8,128)S(1)}, u32[]{:S(2)}) copy-start(f32[512,768]{1,0:T(8,128)S(1)} %fusion.7) | copy-start | bytes 4718596
  8.0 2.6 %copy-start.8 = (f32[512,64]{1,0:T(8,128)}, f32[512,64]{1,0:T(8,128)S(1)}, u32[]{:S(2)}) copy-start(f32[512,64]{1,0:T(8,128)S(1)} %get-tuple-element.24) | copy-start | bytes 393220
  9.8 13.5 %copy-start.10 = (f32[512,128]{1,0:T(8,128)}, f32[512,128]{1,0:T(8,128)S(1)}, u32[]{:S(2)}) copy-start(f32[512,128]{1,0:T(8,128)S(1)} %get-tuple-element.22) | copy-start | bytes 786436
  10.6 8.4 %collective-permute-start = (bf16[512,256]{1,0:T(8,128)(2,1)}, bf16[512,256]{1,0:T(8,128)(2,1)}, u32[]{:S(2)}, u32[]{:S(2)}) collective-permute-start(bf16[512,256]{1,0:T(8,128)(2,1)} %pad_maximum_fusion.6), channel_id=1, source_target_pairs={{0,2},{2,4},{4,6},{6,8},{8,10},{10,12},{12,14},{14,16},{16,18},{18... | collective-permute-start | bytes 786440 | tf_op jit(solution)/shard_map/ppermute | solution.py:19
  19.0 9.4 %copy-start.12 = (f32[512,128]{1,0:T(8,128)S(1)}, f32[512,128]{1,0:T(8,128)}, u32[]{:S(2)}) copy-start(f32[512,128]{1,0:T(8,128)} %get-tuple-element.23) | copy-start | bytes 786436
  19.0 9.6 %copy-start.6 = (f32[512,768]{1,0:T(8,128)S(1)}, f32[512,768]{1,0:T(8,128)}, u32[]{:S(2)}) copy-start(f32[512,768]{1,0:T(8,128)} %copy-done.5) | copy-start | bytes 4718596
  19.0 5.0 %collective-permute-start.1 = (bf16[512,256]{1,0:T(8,128)(2,1)}, bf16[512,256]{1,0:T(8,128)(2,1)S(1)}, u32[]{:S(2)}, u32[]{:S(2)}) collective-permute-start(bf16[512,256]{1,0:T(8,128)(2,1)} %collective-permute-done), channel_id=1, source_target_pairs={{0,2},{2,4},{4,6},{6,8},{8,10},{10,12},{12,14},{14,16},{16,18},{18... | collective-permute-start | bytes 786440 | tf_op jit(solution)/shard_map/ppermute | solution.py:19
  24.0 6.7 %collective-permute-start.2 = (bf16[512,256]{1,0:T(8,128)(2,1)S(1)}, bf16[512,256]{1,0:T(8,128)(2,1)S(1)}, u32[]{:S(2)}, u32[]{:S(2)}) collective-permute-start(bf16[512,256]{1,0:T(8,128)(2,1)S(1)} %collective-permute-done.1), channel_id=1, source_target_pairs={{0,2},{2,4},{4,6},{6,8},{8,10},{10,12},{12,14},{14,16},{16,18},{18... | collective-permute-start | bytes 786440 | tf_op jit(solution)/shard_map/ppermute | solution.py:19
  28.6 1.0 copy-start.3
  54.3 1.3 copy-start
  55.6 0.8 copy-start.2
  58.8 8.5 %collective-permute-start.3 = (bf16[512,256]{1,0:T(8,128)(2,1)S(1)}, bf16[512,256]{1,0:T(8,128)(2,1)S(1)}, u32[]{:S(2)}, u32[]{:S(2)}) collective-permute-start(bf16[512,256]{1,0:T(8,128)(2,1)S(1)} %fusion.16), channel_id=1, source_target_pairs={{2,0},{4,2},{6,4},{8,6},{10,8},{12,10},{14,12},{16,14},{18,16},{20... | collective-permute-start | bytes 786440 | tf_op jit(solution)/shard_map/ppermute | solution.py:19
  60.1 6.9 %copy-start.7 = (f32[512,4,128]{2,1,0:T(4,128)S(1)}, f32[512,4,128]{2,1,0:T(4,128)}, u32[]{:S(2)}) copy-start(f32[512,4,128]{2,1,0:T(4,128)} %reshape.128) | copy-start | bytes 3145732
  60.1 6.9 %copy-start.11 = (f32[512,128]{1,0:T(8,128)S(1)}, f32[512,128]{1,0:T(8,128)}, u32[]{:S(2)}) copy-start(f32[512,128]{1,0:T(8,128)} %copy-done.10) | copy-start | bytes 786436
  60.1 7.2 %copy-start.1 = (f32[4,512,256]{2,1,0:T(8,128)S(1)}, f32[4,512,256]{2,1,0:T(8,128)}, u32[]{:S(2)}) copy-start(f32[4,512,256]{2,1,0:T(8,128)} %copy-done) | copy-start | bytes 6291460
  67.4 12.1 %collective-permute-start.4 = (bf16[512,256]{1,0:T(8,128)(2,1)S(1)}, bf16[512,256]{1,0:T(8,128)(2,1)}, u32[]{:S(2)}, u32[]{:S(2)}) collective-permute-start(bf16[512,256]{1,0:T(8,128)(2,1)S(1)} %fusion.15), channel_id=1, source_target_pairs={{2,0},{4,2},{6,4},{8,6},{10,8},{12,10},{14,12},{16,14},{18,16},{20... | collective-permute-start | bytes 786440 | tf_op jit(solution)/shard_map/ppermute | solution.py:19
  77.2 5.1 %copy-start.4 = (f32[512,4,128]{2,1,0:T(4,128)S(1)}, f32[512,4,128]{2,1,0:T(4,128)}, u32[]{:S(2)}) copy-start(f32[512,4,128]{2,1,0:T(4,128)} %copy-done.3) | copy-start | bytes 3145732
  77.2 11.0 %copy-start.9 = (f32[512,64]{1,0:T(8,128)S(1)}, f32[512,64]{1,0:T(8,128)}, u32[]{:S(2)}) copy-start(f32[512,64]{1,0:T(8,128)} %copy-done.8) | copy-start | bytes 393220
  80.5 9.8 %copy-start.14 = (bf16[1,512,4096]{2,1,0:T(8,128)(2,1)S(1)}, bf16[1,512,4096]{2,1,0:T(8,128)(2,1)}, u32[]{:S(2)}) copy-start(bf16[1,512,4096]{2,1,0:T(8,128)(2,1)} %param.5) | copy-start | bytes 12582916
  80.5 7.6 %collective-permute-start.5 = (bf16[512,256]{1,0:T(8,128)(2,1)S(1)}, bf16[512,256]{1,0:T(8,128)(2,1)S(1)}, u32[]{:S(2)}, u32[]{:S(2)}) collective-permute-start(bf16[512,256]{1,0:T(8,128)(2,1)S(1)} %fusion.14), channel_id=1, source_target_pairs={{2,0},{4,2},{6,4},{8,6},{10,8},{12,10},{14,12},{16,14},{18,16},{20... | collective-permute-start | bytes 786440 | tf_op jit(solution)/shard_map/ppermute | solution.py:19
  89.2 6.6 %slice-start = ((s8[6291456]{0:T(1024)(128)(4,1)}), s8[4194304]{0:T(1024)(128)(4,1)S(1)}, s32[]{:S(2)}) async-start(s8[6291456]{0:T(1024)(128)(4,1)} %bitcast.76), calls=%async_computation | async-start | bytes 8388608
  90.3 5.4 %slice-start.1 = ((s8[6291456]{0:T(1024)(128)(4,1)}), s8[2097152]{0:T(1024)(128)(4,1)S(1)}, s32[]{:S(2)}) async-start(s8[6291456]{0:T(1024)(128)(4,1)} %bitcast.76), calls=%async_computation.1 | async-start | bytes 4194304
where the time goes:
time: 193 us; the launch traced here: 192 us
  Pallas kernels  102 us (53%)
  matrix products  30.2 us (16%)
  local copies, waits for them, and re-layouts  25.2 us (13%)
  starting transfers between devices  14.4 us (7%)
  other arithmetic  13.7 us (7%)
  waiting for transfers between devices  5.46 us (3%)
    pallas_call x1, Pallas kernels, reduce_terms(): pl.pallas_call(reduce_kernel, out_shape=(jax.ShapeDtypeStruct((ROWS, 768)...  79.6 us
    pallas_call x1, Pallas kernels, attention(): pl.pallas_call(attention_kernel, out_shape=(jax.ShapeDtypeStruct((TOK, HE...  22.5 us
    ppermute x6, starting transfers between devices, from_behind(): return lax.ppermute(block, axis, route)  14.4 us
    convert_element_type x1, local copies, waits for them, and re-layouts, per_device(): qkv_term = lax.dot_general(tokens, merged_grad, (((0,), (0,)), ((), ())),...  8.64 us
    dot_general x1, matrix products, per_device(): projected = jnp.dot(tokens, w_qkv, preferred_element_type=jnp.float32)  7.05 us
    dot_general x1, matrix products, per_device(): lax.dot_general(upstream, flat_attended, (((0,), (0,)), ((), ())), prefer...  6.88 us
    convert_element_type x1, local copies, waits for them, and re-layouts, per_device(): out_term = lax.dot_general(upstream, flat_attended, (((0,), (0,)), ((), (...  6.45 us
    unnamed x36, local copies, waits for them, and re-layouts  5.88 us
  transfers between devices with their start and end apart: 6, of which 2 were waited for; matrix products, arithmetic and copies ran while one was open for 14% of the time, Pallas kernels for 0%

commit v1 on v0

--- a/solution.py
+++ b/solution.py
@@ -130,15 +130,9 @@
             device_id_type=MESH_ID,
         )
 
-    def add_into(dst, dst_at, src, src_at, count):
-        def step(k, _):
-            dst[dst_at + (k,)] = (dst[dst_at + (k,)].astype(F32) + src[src_at(k)].astype(F32)).astype(BF16)
-            return 0
-
-        if count == 1:
-            step(0, 0)
-        else:
-            lax.fori_loop(0, count, step, 0)
+    def add_into(dst, dst_at, src, src_at):
+        total = dst[dst_at].astype(F32) + src[src_at].astype(F32)
+        dst[dst_at] = total.astype(BF16)
 
     bufs = ((r1a, r1b), (r2a, r2b), (r3a, r3b))
     sizes = (16, 4, 1)
@@ -175,15 +169,15 @@
             s = second(i)
             src, _ = source(g, stage)
             sends[g, stage, 1].wait_recv()
-            add_into(bufs[stage][0], (g, 1), src, lambda k, s=s, g=g: (g, s * size + k), size)
+            add_into(bufs[stage][0], (g, 1), src, (g, pl.ds(s * size, size)))
             sends[g, stage, 2] = copy(bufs[stage][0].at[g, 1], bufs[stage][1].at[g], g, stage * 3 + 2, moved(order[stage], s))
             sends[g, stage, 2].start()
             sends[g, stage, 0].wait_recv()
-            add_into(bufs[stage][0], (g, 0), src, lambda k, i=i, g=g: (g, i * size + k), size)
+            add_into(bufs[stage][0], (g, 0), src, (g, pl.ds(i * size, size)))
         for g in range(STREAMS):
             sends[g, stage, 2].wait_recv()
             if stage < 2:
-                add_into(bufs[stage][1], (g,), bufs[stage][0], lambda k, g=g: (g, 0, k), size)
+                add_into(bufs[stage][1], (g,), bufs[stage][0], (g, 0))
                 start_first(g, stage + 1)
             else:
                 total = r3b[g, 0].astype(F32) + r3a[g, 0, 0].astype(F32)
@@ -337,10 +331,8 @@
         .reshape(rows_here, HEADS, HEAD)
     )
     received = [key_value]
-    travelling = key_value
     for offset in range(1, SPAN):
-        travelling = from_behind(travelling, "seq", 1)
-        received.append(travelling)
+        received.append(from_behind(key_value, "seq", offset))
     attended, query_grad, kv_terms = attention(
         (device_index * rows_here).reshape(1),
         queries.reshape(rows_here, query_width),
@@ -349,12 +341,9 @@
         query_start.reshape(rows_here, 1),
     )
     query_grad = query_grad.reshape(rows_here, HEADS, HEAD)
-    kv_total = kv_terms[SPAN - 1]
-    for offset in range(SPAN - 2, -1, -1):
-        kv_total = (
-            from_behind(kv_total.astype(jnp.bfloat16), "seq", -1).astype(kv_total.dtype)
-            + kv_terms[offset]
-        )
+    kv_total = kv_terms[0]
+    for offset in range(1, SPAN):
+        kv_total = kv_total + from_behind(kv_terms[offset].astype(BF16), "seq", -offset).astype(F32)
     query_pre = rotate_back(query_grad, cosine_table[:, None, :], sine_table[:, None, :]).reshape(
         rows_here, query_width
     )

time: 193 us -> 171 us (0.89)
  Pallas kernels: 102 us -> 83.1 us
  waiting for transfers between devices: 5.46 us -> 0.02 us
  local copies, waits for them, and re-layouts: 25.2 us -> 28.5 us
  matrix products: 30.2 us -> 27.1 us
  other arithmetic: 13.7 us -> 16.5 us
    pallas_call x1, Pallas kernels: 79.6 us -> 60.6 us  [reduce_terms(): pl.pallas_call(reduce_kernel, out_shape=(jax.ShapeDtypeStruct((ROWS, 768)...]
    ppermute x6, waiting for transfers between devices: 5.46 us -> 0.02 us  [from_behind(): return lax.ppermute(block, axis, route)]
    dot_general x1, matrix products: 6.88 us -> 4.39 us  [per_device(): lax.dot_general(upstream, flat_attended, (((0,), (0,)), ((), ())), prefer...]
    unnamed x36 -> x30, local copies, waits for them, and re-layouts: 5.88 us -> 8.18 us
    another operation x3 -> x4, other arithmetic: 3.23 us -> 3.96 us
  transfers between devices with their start and end apart: 6 -> 6, of which waited for: 2 -> 0; matrix products, arithmetic and copies ran while one was open for 14% -> 15% of each run, Pallas kernels for 0% -> 0%
where the time goes in v1:
time: 171 us
  Pallas kernels  83.1 us (49%)
  local copies, waits for them, and re-layouts  28.5 us (17%)
  matrix products  27.1 us (16%)
  other arithmetic  16.5 us (10%)
  starting transfers between devices  14.2 us (8%)
    pallas_call x1, Pallas kernels, reduce_terms(): pl.pallas_call(reduce_kernel, out_shape=(jax.ShapeDtypeStruct((ROWS, 768)...  60.6 us
    pallas_call x1, Pallas kernels, attention(): pl.pallas_call(attention_kernel, out_shape=(jax.ShapeDtypeStruct((TOK, HE...  22.5 us
    ppermute x6, starting transfers between devices, from_behind(): return lax.ppermute(block, axis, route)  14.2 us
    convert_element_type x1, local copies, waits for them, and re-layouts, per_device(): qkv_term = lax.dot_general(tokens, merged_grad, (((0,), (0,)), ((), ())),...  8.63 us
    unnamed x30, local copies, waits for them, and re-layouts  8.18 us
    dot_general x1, matrix products, per_device(): projected = jnp.dot(tokens, w_qkv, preferred_element_type=jnp.float32)  7.05 us
    convert_element_type x1, local copies, waits for them, and re-layouts, per_device(): out_term = lax.dot_general(upstream, flat_attended, (((0,), (0,)), ((), (...  6.45 us
    dot_general x1, matrix products, per_device(): lax.dot_general(tokens, merged_grad, (((0,), (0,)), ((), ())), preferred_...  5.35 us
  transfers between devices with their start and end apart: 6, of which 0 were waited for; matrix products, arithmetic and copies ran while one was open for 15% of the time, Pallas kernels for 0%

profile of v1, /device:TPU:0, one launch (start us, length us, event | category | flops | bytes accessed | tf_op | source)
XLA Modules:
  0.0 170.6 jit_solution(3640052667795944850)
XLA Ops:
  0.7 7.0 %fusion.7 = f32[512,768]{1,0:T(8,128)S(1)} fusion(bf16[4096,768]{1,0:T(8,128)(2,1)} %param.7, bf16[1,512,4096]{2,1,0:T(8,128)(2,1)} %param.5), kind=kOutput, calls=%fused_computation.10 | convolution fusion | flops 3221225472 | bytes 12058624 | tf_op jit(solution)/shard_map/dot_general | solution.py:316
  7.8 0.2 slice_negate_fusion.3
  8.0 0.7 copy-done.7
  8.7 1.2 fusion.17
  9.9 0.8 pad_maximum_fusion.6
  10.6 2.0 %collective-permute-start = (bf16[512,256]{1,0:T(8,128)(2,1)}, bf16[512,256]{1,0:T(8,128)(2,1)}, u32[]{:S(2)}, u32[]{:S(2)}) collective-permute-start(bf16[512,256]{1,0:T(8,128)(2,1)} %pad_maximum_fusion.6), channel_id=1, source_target_pairs={{0,2},{2,4},{4,6},{6,8},{8,10},{10,12},{12,14},{14,16},{16,18},{18... | collective-permute-start | bytes 786440 | tf_op jit(solution)/shard_map/ppermute | solution.py:19
  12.7 4.1 %collective-permute-start.1 = (bf16[512,256]{1,0:T(8,128)(2,1)}, bf16[512,256]{1,0:T(8,128)(2,1)}, u32[]{:S(2)}, u32[]{:S(2)}) collective-permute-start(bf16[512,256]{1,0:T(8,128)(2,1)} %pad_maximum_fusion.6), channel_id=1, source_target_pairs={{0,4},{2,6},{4,8},{6,10},{8,12},{10,14},{12,16},{14,18},{16,20},{1... | collective-permute-start | bytes 786440 | tf_op jit(solution)/shard_map/ppermute | solution.py:19
  16.8 4.0 %collective-permute-start.2 = (bf16[512,256]{1,0:T(8,128)(2,1)}, bf16[512,256]{1,0:T(8,128)(2,1)}, u32[]{:S(2)}, u32[]{:S(2)}) collective-permute-start(bf16[512,256]{1,0:T(8,128)(2,1)} %pad_maximum_fusion.6), channel_id=1, source_target_pairs={{0,6},{2,8},{4,10},{6,12},{8,14},{10,16},{12,18},{14,20},{16,22},{... | collective-permute-start | bytes 786440 | tf_op jit(solution)/shard_map/ppermute | solution.py:19
  20.8 1.1 slice.74
  21.9 1.6 reshape.129
  23.5 0.6 slice_negate_fusion.1
  24.1 1.6 copy-done.5
  25.7 5.3 %fusion.9.g_ref = bf16[512,512]{1,0:T(8,128)(2,1)} fusion(bf16[512,4096]{1,0:T(8,128)(2,1)} %param.8, bf16[1,512,4096]{2,1,0:T(8,128)(2,1)S(1)} %copy-done.5), kind=kOutput, calls=%fused_computation.12 | convolution fusion | flops 2147745792 | bytes 8912896 | tf_op jit(solution)/shard_map/dot_general | solution.py:327
  31.0 0.7 maximum_multiply_fusion
  31.7 0.2 mul.77
  31.9 1.1 fusion.13.q_ref
  33.0 0.1 copy.10.start_ref
  33.2 1.2 pad_maximum_fusion.kv_ref
  34.4 0.0 copy-start
  34.4 1.0 copy-done
  35.5 1.0 copy-done.3
  36.5 22.5 %shard_map.76 = (bf16[512,512]{1,0:T(8,128)(2,1)S(1)}, f32[512,512]{1,0:T(8,128)S(1)}, f32[4,512,256]{2,1,0:T(8,128)S(1)}) custom-call(s32[1]{0:T(128)} %bitcast.first_ref, bf16[512,512]{1,0:T(8,128)(2,1)S(1)} %copy-done, bf16[512,512]{1,0:T(8,128)(2,1)S(1)} %copy-done.3, bf16[4,512,256]{2,1,0:T(8,128)(2,1)S(1)} %pad_maximum_fusion.kv_ref, ...), custom_call_target="tpu_custom_call" | custom-call | tf_op jit(solution)/shard_map/pallas_call | solution.py:293
  59.0 0.8 copy-done.1
  59.8 1.3 reshape.130
  61.1 1.5 broadcast_multiply_fusion
  62.7 2.1 %fusion.23 = (f32[512,4,64]{2,1,0:T(4,128)}, f32[512,4,64]{2,1,0:T(4,128)}) fusion(f32[512,4,128]{2,1,0:T(4,128)S(1)} %broadcast_multiply_fusion), kind=kLoop, calls=%fused_computation.52 | loop fusion | flops 131072 | bytes 2097152 | tf_op jit(solution)/shard_map/slice | solution.py:40
  64.7 0.1 convert.28
  64.8 0.9 slice_bitcast_fusion.2
  65.7 1.3 collective-permute-start.3
  67.0 1.3 collective-permute-start.4
  68.3 1.5 collective-permute-start.5
  69.8 4.4 %fusion.1 = bf16[4096,512]{0,1:T(8,128)(2,1)} fusion(bf16[512,512]{1,0:T(8,128)(2,1)S(1)} %copy-done.2, bf16[1,512,4096]{2,1,0:T(8,128)(2,1)S(1)} %copy-done.6), kind=kOutput, calls=%fused_computation.4 | convolution fusion | flops 2149580800 | bytes 8912896 | tf_op jit(solution)/shard_map/dot_general | solution.py:358
  74.2 6.5 %copy.12 = bf16[4096,512]{1,0:T(8,128)(2,1)} copy(bf16[4096,512]{0,1:T(8,128)(2,1)} %fusion.1) | data formatting | bytes 8388608 | tf_op jit(solution)/shard_map/convert_element_type | solution.py:360
  80.7 2.2 %pad_maximum_fusion.1 = f32[512,4,128]{2,1,0:T(4,128)S(1)} fusion(f32[512,4,64]{2,1,0:T(4,128)} %get-tuple-element.16, f32[512,4,64]{2,1,0:T(4,128)} %get-tuple-element.15), kind=kLoop, calls=%fused_computation.23 | loop fusion | flops 262144 | bytes 2097152 | tf_op jit(solution)/shard_map/concatenate | solution.py:39
  82.9 0.0 copy-start.11
  82.9 1.7 fusion.12
  84.6 1.1 fusion.15
  85.7 0.9 slice_multiply_fusion.1
  86.7 0.0 slice-start
  86.7 0.1 fusion.24
  86.9 1.0 fusion.18
  87.9 0.0 slice-start.1
  87.9 5.4 %fusion = bf16[4096,768]{0,1:T(8,128)(2,1)} fusion(bf16[1,512,4096]{2,1,0:T(8,128)(2,1)S(1)} %copy-done.11, bf16[512,128]{1,0:T(8,128)(2,1)S(1)} %slice.108, bf16[512,128]{1,0:T(8,128)(2,1)S(1)} %fusion.18, bf16[512,512]{1,0:T(8,128)(2,1)S(1)} %fusion.12), kind=kOutput, calls=%fused_computation.1 | convolution fusion | flops 3226730496 | bytes 11272192 | tf_op jit(solution)/shard_map/dot_general | solution.py:361
  93.3 5.0 %fusion.2 = bf16[1,512,4096]{2,1,0:T(8,128)(2,1)} fusion(bf16[4096,768]{1,0:T(8,128)(2,1)S(1)} %bitcast.75, bf16[512,128]{1,0:T(8,128)(2,1)S(1)} %slice.108, bf16[512,128]{1,0:T(8,128)(2,1)S(1)} %fusion.18, bf16[512,512]{1,0:T(8,128)(2,1)S(1)} %fusion.12), kind=kOutput, calls=%fused_computation.5 | convolution fusion | flops 3225681920 | bytes 11272192 | tf_op jit(solution)/shard_map/dot_general | solution.py:354
  98.3 8.6 %copy.11 = bf16[4096,768]{1,0:T(8,128)(2,1)} copy(bf16[4096,768]{0,1:T(8,128)(2,1)} %fusion) | data formatting | bytes 12582912 | tf_op jit(solution)/shard_map/convert_element_type | solution.py:363
  106.9 60.6 %shard_map.77 = (f32[32,768]{1,0:T(8,128)}, f32[32,512]{1,0:T(8,128)}) custom-call(bf16[32,2,64,768]{3,2,1,0:T(8,128)(2,1)} %bitcast.64, bf16[32,2,64,512]{3,2,1,0:T(8,128)(2,1)} %bitcast.65), custom_call_target="tpu_custom_call" | custom-call | tf_op jit(solution)/shard_map/pallas_call | solution.py:197
  167.5 1.5 copy.22
  169.1 1.5 copy.23
  (31 shorter events, 0.1 us)
Async XLA Ops:
  0.7 7.1 %copy-start.10 = (s32[1,512]{1,0:T(1,128)S(1)}, s32[1,512]{1,0:T(1,128)}, u32[]{:S(2)}) copy-start(s32[1,512]{1,0:T(1,128)} %param.9) | copy-start | bytes 6148
  8.0 0.7 copy-start.7
  9.8 21.2 %copy-start.9 = (f32[512,128]{1,0:T(8,128)}, f32[512,128]{1,0:T(8,128)S(1)}, u32[]{:S(2)}) copy-start(f32[512,128]{1,0:T(8,128)S(1)} %get-tuple-element.25) | copy-start | bytes 786436
  10.6 22.5 %collective-permute-start = (bf16[512,256]{1,0:T(8,128)(2,1)}, bf16[512,256]{1,0:T(8,128)(2,1)}, u32[]{:S(2)}, u32[]{:S(2)}) collective-permute-start(bf16[512,256]{1,0:T(8,128)(2,1)} %pad_maximum_fusion.6), channel_id=1, source_target_pairs={{0,2},{2,4},{4,6},{6,8},{8,10},{10,12},{12,14},{14,16},{16,18},{18... | collective-permute-start | bytes 786440 | tf_op jit(solution)/shard_map/ppermute | solution.py:19
  12.7 20.5 %collective-permute-start.1 = (bf16[512,256]{1,0:T(8,128)(2,1)}, bf16[512,256]{1,0:T(8,128)(2,1)}, u32[]{:S(2)}, u32[]{:S(2)}) collective-permute-start(bf16[512,256]{1,0:T(8,128)(2,1)} %pad_maximum_fusion.6), channel_id=1, source_target_pairs={{0,4},{2,6},{4,8},{6,10},{8,12},{10,14},{12,16},{14,18},{16,20},{1... | collective-permute-start | bytes 786440 | tf_op jit(solution)/shard_map/ppermute | solution.py:19
  16.8 16.4 %collective-permute-start.2 = (bf16[512,256]{1,0:T(8,128)(2,1)}, bf16[512,256]{1,0:T(8,128)(2,1)}, u32[]{:S(2)}, u32[]{:S(2)}) collective-permute-start(bf16[512,256]{1,0:T(8,128)(2,1)} %pad_maximum_fusion.6), channel_id=1, source_target_pairs={{0,6},{2,8},{4,10},{6,12},{8,14},{10,16},{12,18},{14,20},{16,22},{... | collective-permute-start | bytes 786440 | tf_op jit(solution)/shard_map/ppermute | solution.py:19
  23.5 2.2 %copy-start.5 = (bf16[1,512,4096]{2,1,0:T(8,128)(2,1)S(1)}, bf16[1,512,4096]{2,1,0:T(8,128)(2,1)}, u32[]{:S(2)}) copy-start(bf16[1,512,4096]{2,1,0:T(8,128)(2,1)} %param.6) | copy-start | bytes 12582916
  31.9 1.1 copy-start.4
  34.4 1.0 copy-start
  35.5 1.0 copy-start.3
  59.0 0.8 copy-start.1
  62.6 7.2 %copy-start.2 = (bf16[512,512]{1,0:T(8,128)(2,1)S(1)}, bf16[512,512]{1,0:T(8,128)(2,1)}, u32[]{:S(2)}) copy-start(bf16[512,512]{1,0:T(8,128)(2,1)} %copy-done.1) | copy-start | bytes 1572868
  62.6 7.2 %copy-start.6 = (bf16[1,512,4096]{2,1,0:T(8,128)(2,1)S(1)}, bf16[1,512,4096]{2,1,0:T(8,128)(2,1)}, u32[]{:S(2)}) copy-start(bf16[1,512,4096]{2,1,0:T(8,128)(2,1)} %param.6) | copy-start | bytes 12582916
  65.7 18.9 %collective-permute-start.3 = (bf16[512,256]{1,0:T(8,128)(2,1)}, bf16[512,256]{1,0:T(8,128)(2,1)S(1)}, u32[]{:S(2)}, u32[]{:S(2)}) collective-permute-start(bf16[512,256]{1,0:T(8,128)(2,1)} %get-tuple-element.17), channel_id=1, source_target_pairs={{2,0},{4,2},{6,4},{8,6},{10,8},{12,10},{14,12},{16,14},{18,16},{20... | collective-permute-start | bytes 786440 | tf_op jit(solution)/shard_map/ppermute | solution.py:19
  67.0 17.6 %collective-permute-start.4 = (bf16[512,256]{1,0:T(8,128)(2,1)}, bf16[512,256]{1,0:T(8,128)(2,1)}, u32[]{:S(2)}, u32[]{:S(2)}) collective-permute-start(bf16[512,256]{1,0:T(8,128)(2,1)} %get-tuple-element.19), channel_id=1, source_target_pairs={{4,0},{6,2},{8,4},{10,6},{12,8},{14,10},{16,12},{18,14},{20,16},{2... | collective-permute-start | bytes 786440 | tf_op jit(solution)/shard_map/ppermute | solution.py:19
  68.3 16.3 %collective-permute-start.5 = (bf16[512,256]{1,0:T(8,128)(2,1)}, bf16[512,256]{1,0:T(8,128)(2,1)}, u32[]{:S(2)}, u32[]{:S(2)}) collective-permute-start(bf16[512,256]{1,0:T(8,128)(2,1)} %get-tuple-element.18), channel_id=1, source_target_pairs={{6,0},{8,2},{10,4},{12,6},{14,8},{16,10},{18,12},{20,14},{22,16},{... | collective-permute-start | bytes 786440 | tf_op jit(solution)/shard_map/ppermute | solution.py:19
  80.7 5.1 %copy-start.8 = (f32[512,64]{1,0:T(8,128)S(1)}, f32[512,64]{1,0:T(8,128)}, u32[]{:S(2)}) copy-start(f32[512,64]{1,0:T(8,128)} %copy-done.7) | copy-start | bytes 393220
  82.9 5.0 %copy-start.11 = (bf16[1,512,4096]{2,1,0:T(8,128)(2,1)S(1)}, bf16[1,512,4096]{2,1,0:T(8,128)(2,1)}, u32[]{:S(2)}) copy-start(bf16[1,512,4096]{2,1,0:T(8,128)(2,1)} %param.5) | copy-start | bytes 12582916
  86.7 6.5 %slice-start = ((s8[6291456]{0:T(1024)(128)(4,1)}), s8[4194304]{0:T(1024)(128)(4,1)S(1)}, s32[]{:S(2)}) async-start(s8[6291456]{0:T(1024)(128)(4,1)} %bitcast.74), calls=%async_computation | async-start | bytes 8388608
  87.9 5.4 %slice-start.1 = ((s8[6291456]{0:T(1024)(128)(4,1)}), s8[2097152]{0:T(1024)(128)(4,1)S(1)}, s32[]{:S(2)}) async-start(s8[6291456]{0:T(1024)(128)(4,1)} %bitcast.74), calls=%async_computation.1 | async-start | bytes 4194304

commit v2 on v1

--- a/solution.py
+++ b/solution.py
@@ -45,6 +45,9 @@
 ROWS = 32
 LANES = 128
 STREAMS = 10
+Q_STREAMS = tuple(range(6))
+O_STREAMS = tuple(range(6, 10))
+CHUNKS = 4
 BF16 = jnp.bfloat16
 F32 = jnp.float32
 MESH_ID = pl.DeviceIdType.MESH
@@ -68,7 +71,7 @@
     return ((((y // 2) * AXES + z) * AXES + x) * 2 + core, y % 2)
 
 
-def reduce_kernel(q_ref, o_ref, q_out, o_out, q_in, o_in, held, r1a, r1b, r2a, r2b, r3a, r3b, sib_sem, send_sem, recv_sem):
+def reduce_kernel(tok_ref, mg_ref, o_ref, q_out, o_out, q_ref, q_in, o_in, held, r1a, r1b, r2a, r2b, r3a, r3b, sib_sem, send_sem, recv_sem):
     seq = lax.axis_index("seq")
     dp = lax.axis_index("dp")
     core = seq % 2
@@ -85,40 +88,48 @@
     for axis in range(3):
         for pair in (even_pair, odd_pair):
             pl.semaphore_signal(barrier, inc=1, device_id=moved(axis, pair(here[axis])), device_id_type=MESH_ID)
-    pl.semaphore_wait(barrier, 7)
-
-    swaps = []
-    for n, (src, dst) in enumerate(((q_ref, q_in), (o_ref, o_in))):
-        swap = pltpu.make_async_remote_copy(
-            src_ref=src.at[:, 1 - core],
+
+    span = 2 * AXES * AXES // CHUNKS
+
+    def multiply(chunk):
+        def pair(k, _):
+            at = chunk * span + 2 * k
+            cols = pl.ds(pl.multiple_of(at * 4 * ROWS, 8 * ROWS), 8 * ROWS)
+            term = mm(tok_ref[:, cols], mg_ref[...], TN).astype(BF16)
+            q_ref[pl.ds(at, 2)] = term.reshape(2, 2, 2 * ROWS, 768)
+            return 0
+
+        lax.fori_loop(0, span // 2, pair, 0)
+
+    def swap(n, src, dst):
+        return pltpu.make_async_remote_copy(
+            src_ref=src,
             dst_ref=dst,
             send_sem=sib_sem.at[0, n],
             recv_sem=sib_sem.at[1, n],
             device_id=sibling,
             device_id_type=MESH_ID,
         )
-        swap.start()
-        swaps.append(swap)
-    for swap in swaps:
-        swap.wait_recv()
-
-    def combine(block, _):
-        y_hi = block // 16
-        z = (block // 4) % 4
-        x = block % 4
-        for y_lo in range(2):
-            spot = (x, y_hi * 2 + y_lo, z)
-            rows = slice(y_lo * ROWS, (y_lo + 1) * ROWS)
-            for g in range(STREAMS):
-                order, _, _ = stream_plan(g)
-                place = (spot[order[0]] * AXES + spot[order[1]]) * AXES + spot[order[2]]
-                src, got, col = (q_ref, q_in, g) if g < 6 else (o_ref, o_in, g - 6)
-                cols = slice(col * LANES, (col + 1) * LANES)
-                total = src[block, core, rows, cols].astype(F32) + got[block, rows, cols].astype(F32)
-                held[g, place] = total.astype(BF16)
-        return 0
-
-    lax.fori_loop(0, 32, combine, 0)
+
+    def combine(own, got, streams, start, count):
+        def step(k, _):
+            block = start + k
+            y_hi = block // 16
+            z = (block // 4) % 4
+            x = block % 4
+            for y_lo in range(2):
+                spot = (x, y_hi * 2 + y_lo, z)
+                rows = slice(y_lo * ROWS, (y_lo + 1) * ROWS)
+                for g in streams:
+                    order, _, _ = stream_plan(g)
+                    place = (spot[order[0]] * AXES + spot[order[1]]) * AXES + spot[order[2]]
+                    col = g - streams[0]
+                    cols = slice(col * LANES, (col + 1) * LANES)
+                    total = own[block, core, rows, cols].astype(F32) + got[block, rows, cols].astype(F32)
+                    held[g, place] = total.astype(BF16)
+            return 0
+
+        lax.fori_loop(0, count, step, 0)
 
     def copy(src, dst, g, n, target):
         return pltpu.make_async_remote_copy(
@@ -159,11 +170,29 @@
             )
             sends[g, stage, slot].start()
 
-    for g in range(STREAMS):
+    swaps = []
+    for chunk in range(CHUNKS):
+        multiply(chunk)
+        if chunk == 0:
+            pl.semaphore_wait(barrier, 7)
+            swaps.append(swap(CHUNKS, o_ref.at[:, 1 - core], o_in))
+            swaps[0].start()
+        part = pl.ds(chunk * span, span)
+        swaps.append(swap(chunk, q_ref.at[part, 1 - core], q_in.at[part]))
+        swaps[-1].start()
+        if chunk == 1:
+            swaps[0].wait_recv()
+            combine(o_ref, o_in, O_STREAMS, 0, 2 * AXES * AXES)
+            for g in O_STREAMS:
+                start_first(g, 0)
+    for chunk in range(CHUNKS):
+        swaps[1 + chunk].wait_recv()
+        combine(q_ref, q_in, Q_STREAMS, chunk * span, span)
+    for g in Q_STREAMS:
         start_first(g, 0)
     for stage in range(3):
         size = sizes[stage]
-        for g in range(STREAMS):
+        for g in O_STREAMS + Q_STREAMS:
             order, first, second = stream_plan(g)
             i = here[order[stage]]
             s = second(i)
@@ -174,7 +203,7 @@
             sends[g, stage, 2].start()
             sends[g, stage, 0].wait_recv()
             add_into(bufs[stage][0], (g, 0), src, (g, pl.ds(i * size, size)))
-        for g in range(STREAMS):
+        for g in O_STREAMS + Q_STREAMS:
             sends[g, stage, 2].wait_recv()
             if stage < 2:
                 add_into(bufs[stage][1], (g,), bufs[stage][0], (g, 0))
@@ -185,13 +214,13 @@
                     q_out[:, g * LANES : (g + 1) * LANES] = total
                 else:
                     o_out[:, (g - 6) * LANES : (g - 5) * LANES] = total
-    for swap in swaps:
-        swap.wait_send()
+    for item in swaps:
+        item.wait_send()
     for send in sends.values():
         send.wait_send()
 
 
-def reduce_terms(q_term, o_term):
+def reduce_terms(tokens, merged_grad, o_term):
     vmem = pl.BlockSpec(memory_space=pltpu.VMEM)
     tile = (ROWS, LANES)
     return pl.pallas_call(
@@ -200,9 +229,10 @@
             jax.ShapeDtypeStruct((ROWS, 768), F32),
             jax.ShapeDtypeStruct((ROWS, 512), F32),
         ),
-        in_specs=[vmem, vmem],
+        in_specs=[vmem, vmem, vmem],
         out_specs=(vmem, vmem),
         scratch_shapes=[
+            pltpu.VMEM((32, 2, 2 * ROWS, 768), BF16),
             pltpu.VMEM((32, 2 * ROWS, 768), BF16),
             pltpu.VMEM((32, 2 * ROWS, 512), BF16),
             pltpu.VMEM((STREAMS, 64) + tile, BF16),
@@ -212,14 +242,14 @@
             pltpu.VMEM((STREAMS, 4) + tile, BF16),
             pltpu.VMEM((STREAMS, 2, 1) + tile, BF16),
             pltpu.VMEM((STREAMS, 1) + tile, BF16),
-            pltpu.SemaphoreType.DMA((2, 2)),
+            pltpu.SemaphoreType.DMA((2, CHUNKS + 1)),
             pltpu.SemaphoreType.DMA((STREAMS, 9)),
             pltpu.SemaphoreType.DMA((STREAMS, 9)),
         ],
         compiler_params=pltpu.CompilerParams(
             collective_id=0, has_side_effects=True, vmem_limit_bytes=60 * 1024 * 1024
         ),
-    )(q_term.reshape(32, 2, 2 * ROWS, 768), o_term.reshape(32, 2, 2 * ROWS, 512))
+    )(tokens, merged_grad, o_term.reshape(32, 2, 2 * ROWS, 512))
 
 
 NT = (((1,), (1,)), ((), ()))
@@ -303,6 +333,31 @@
     )(first, q, g, kv, start)
 
 
+def out_kernel(g_ref, att_ref, term_ref):
+    term_ref[...] = mm(g_ref[...], att_ref[...], TN).astype(BF16)
+
+
+def out_terms(upstream, attended):
+    rows, width = upstream.shape
+    cols = attended.shape[1]
+    step = 512
+    return pl.pallas_call(
+        out_kernel,
+        grid=(width // step,),
+        out_shape=jax.ShapeDtypeStruct((width, cols), BF16),
+        in_specs=[
+            pl.BlockSpec((rows, step), lambda i: (0, i)),
+            pl.BlockSpec((rows, cols), lambda i: (0, 0)),
+        ],
+        out_specs=pl.BlockSpec((step, cols), lambda i: (i, 0)),
+        cost_estimate=pl.CostEstimate(
+            flops=2 * rows * width * cols,
+            bytes_accessed=2 * (rows * width + rows * cols + width * cols),
+            transcendentals=0,
+        ),
+    )(upstream, attended)
+
+
 def per_device(inputs, cotangent, w_qkv, w_out, doc_start):
     tokens = inputs[0]
     upstream = cotangent[0]
@@ -355,13 +410,8 @@
         merged_grad, w_qkv, (((1,), (1,)), ((), ())), preferred_element_type=jnp.float32
     ).astype(jnp.bfloat16)[None]
     flat_attended = attended.reshape(rows_here, query_width)
-    out_term = lax.dot_general(
-        upstream, flat_attended, (((0,), (0,)), ((), ())), preferred_element_type=jnp.float32
-    ).astype(jnp.bfloat16)
-    qkv_term = lax.dot_general(
-        tokens, merged_grad, (((0,), (0,)), ((), ())), preferred_element_type=jnp.float32
-    ).astype(jnp.bfloat16)
-    qkv_grad, out_rows = reduce_terms(qkv_term, out_term)
+    out_term = out_terms(upstream, flat_attended)
+    qkv_grad, out_rows = reduce_terms(tokens, merged_grad, out_term)
     out_grad = out_rows.T
     return (input_grad, qkv_grad, out_grad)
 

time: 171 us -> 153 us (0.89)
  local copies, waits for them, and re-layouts: 28.5 us -> 12.4 us
  matrix products: 27.1 us -> 20.2 us
  Pallas kernels: 83.1 us -> 86.9 us
    convert_element_type x2 -> x0, local copies, waits for them, and re-layouts: 15.1 us -> none  [the longest x1 8.63 us: per_device(): qkv_term = lax.dot_general(tokens, merged_grad, (((0,), (0,)), ((), ())),...]
    dot_general x2 -> x0, matrix products: 9.74 us -> none  [the longest x1 5.35 us: per_device(): lax.dot_general(tokens, merged_grad, (((0,), (0,)), ((), ())), preferred_...]
    pallas_call x0 -> x1, Pallas kernels: none -> 8.29 us  [out_terms(): pl.pallas_call(out_kernel, grid=(width // step,), out_shape=jax.ShapeDtyp...]
    pallas_call x1, Pallas kernels: 60.6 us -> 56.1 us  [reduce_terms(): pl.pallas_call(reduce_kernel, out_shape=(jax.ShapeDtypeStruct((ROWS, 768)...]
    dot_general x1, matrix products: 5 us -> 7.79 us  [per_device(): lax.dot_general(merged_grad, w_qkv, (((1,), (1,)), ((), ())), preferred_e...]
    unnamed x30 -> x22, local copies, waits for them, and re-layouts: 8.18 us -> 7.11 us
  transfers between devices with their start and end apart: 6 -> 6, of which waited for: 0 -> 2; matrix products, arithmetic and copies ran while one was open for 15% -> 9% of each run, Pallas kernels for 0% -> 5%
where the time goes in v2:
time: 153 us; the launch traced here: 152 us
  Pallas kernels  86.9 us (57%)
  matrix products  20.2 us (13%)
  other arithmetic  15.8 us (10%)
  starting transfers between devices  14.2 us (9%)
  local copies, waits for them, and re-layouts  12.4 us (8%)
    pallas_call x1, Pallas kernels, reduce_terms(): pl.pallas_call(reduce_kernel, out_shape=(jax.ShapeDtypeStruct((ROWS, 768)...  56.1 us
    pallas_call x1, Pallas kernels, attention(): pl.pallas_call(attention_kernel, out_shape=(jax.ShapeDtypeStruct((TOK, HE...  22.5 us
    ppermute x6, starting transfers between devices, from_behind(): return lax.ppermute(block, axis, route)  14.2 us
    pallas_call x1, Pallas kernels, out_terms(): pl.pallas_call(out_kernel, grid=(width // step,), out_shape=jax.ShapeDtyp...  8.29 us
    dot_general x1, matrix products, per_device(): lax.dot_general(merged_grad, w_qkv, (((1,), (1,)), ((), ())), preferred_e...  7.79 us
    unnamed x22, local copies, waits for them, and re-layouts  7.11 us
    dot_general x1, matrix products, per_device(): projected = jnp.dot(tokens, w_qkv, preferred_element_type=jnp.float32)  7.05 us
    dot_general x1, matrix products, per_device(): lax.dot_general(upstream, w_out, (((1,), (1,)), ((), ())), preferred_elem...  5.35 us
  transfers between devices with their start and end apart: 6, of which 2 were waited for; matrix products, arithmetic and copies ran while one was open for 9% of the time, Pallas kernels for 5%

profile of v2, /device:TPU:0, one launch (start us, length us, event | category | flops | bytes accessed | tf_op | source)
XLA Modules:
  0.0 151.9 jit_solution(15951102209667854053)
XLA Ops:
  0.7 0.0 copy-start.9
  0.7 7.0 %fusion.11 = f32[512,768]{1,0:T(8,128)S(1)} fusion(bf16[4096,768]{1,0:T(8,128)(2,1)} %param.7, bf16[1,512,4096]{2,1,0:T(8,128)(2,1)} %param.5), kind=kOutput, calls=%fused_computation.41 | convolution fusion | flops 3221225472 | bytes 12058624 | tf_op jit(solution)/shard_map/dot_general | solution.py:371
  7.8 0.2 slice_negate_fusion.3
  8.0 0.7 copy-done.5
  8.7 1.2 fusion.6
  9.9 0.8 pad_maximum_fusion.4
  10.7 2.0 %collective-permute-start = (bf16[512,256]{1,0:T(8,128)(2,1)}, bf16[512,256]{1,0:T(8,128)(2,1)}, u32[]{:S(2)}, u32[]{:S(2)}) collective-permute-start(bf16[512,256]{1,0:T(8,128)(2,1)} %pad_maximum_fusion.4), channel_id=1, source_target_pairs={{0,2},{2,4},{4,6},{6,8},{8,10},{10,12},{12,14},{14,16},{16,18},{18... | collective-permute-start | bytes 786440 | tf_op jit(solution)/shard_map/ppermute | solution.py:19
  12.6 4.1 %collective-permute-start.1 = (bf16[512,256]{1,0:T(8,128)(2,1)}, bf16[512,256]{1,0:T(8,128)(2,1)}, u32[]{:S(2)}, u32[]{:S(2)}) collective-permute-start(bf16[512,256]{1,0:T(8,128)(2,1)} %pad_maximum_fusion.4), channel_id=1, source_target_pairs={{0,4},{2,6},{4,8},{6,10},{8,12},{10,14},{12,16},{14,18},{16,20},{1... | collective-permute-start | bytes 786440 | tf_op jit(solution)/shard_map/ppermute | solution.py:19
  16.8 4.0 %collective-permute-start.2 = (bf16[512,256]{1,0:T(8,128)(2,1)}, bf16[512,256]{1,0:T(8,128)(2,1)}, u32[]{:S(2)}, u32[]{:S(2)}) collective-permute-start(bf16[512,256]{1,0:T(8,128)(2,1)} %pad_maximum_fusion.4), channel_id=1, source_target_pairs={{0,6},{2,8},{4,10},{6,12},{8,14},{10,16},{12,18},{14,20},{16,22},{... | collective-permute-start | bytes 786440 | tf_op jit(solution)/shard_map/ppermute | solution.py:19
  20.8 1.1 slice.74
  21.9 1.6 %reshape.126 = f32[512,4,128]{2,1,0:T(4,128)S(1)} reshape(f32[512,512]{1,0:T(8,128)} %slice.74) | data formatting | bytes 2097152 | tf_op jit(solution)/shard_map/reshape | solution.py:373
  23.5 0.0 copy-start.4
  23.5 0.6 slice_negate_fusion.1
  24.1 1.6 %copy-done.4 = bf16[1,512,4096]{2,1,0:T(8,128)(2,1)S(1)} copy-done((bf16[1,512,4096]{2,1,0:T(8,128)(2,1)S(1)}, bf16[1,512,4096]{2,1,0:T(8,128)(2,1)}, u32[]{:S(2)}) %copy-start.4) | copy-done | bytes 4194328
  25.7 5.3 %convolution_convert_fusion.1.g_ref = bf16[512,512]{1,0:T(8,128)(2,1)} fusion(bf16[512,4096]{1,0:T(8,128)(2,1)} %param.8, bf16[1,512,4096]{2,1,0:T(8,128)(2,1)S(1)} %copy-done.4), kind=kOutput, calls=%fused_computation.2 | convolution fusion | flops 2147745792 | bytes 8912896 | tf_op jit(solution)/shard_map/dot_general | solution.py:382
  31.0 0.7 maximum_multiply_fusion
  31.7 0.2 mul.77
  31.9 1.1 fusion.2.q_ref
  33.0 0.1 copy.8.start_ref
  33.2 0.0 copy-start
  33.2 0.0 collective-permute-done
  33.2 0.0 collective-permute-done.1
  33.2 1.2 pad_maximum_fusion.kv_ref
  34.5 1.0 copy-done.2
  35.5 22.5 %shard_map.76 = (bf16[512,512]{1,0:T(8,128)(2,1)S(1)}, f32[512,512]{1,0:T(8,128)S(1)}, f32[4,512,256]{2,1,0:T(8,128)S(1)}) custom-call(s32[1]{0:T(128)} %bitcast.first_ref, bf16[512,512]{1,0:T(8,128)(2,1)S(1)} %copy-done, bf16[512,512]{1,0:T(8,128)(2,1)S(1)} %copy-done.2, bf16[4,512,256]{2,1,0:T(8,128)(2,1)S(1)} %pad_maximum_fusion.kv_ref, ...), custom_call_target="tpu_custom_call" | custom-call | tf_op jit(solution)/shard_map/pallas_call | solution.py:323
  58.0 0.8 copy-done.1
  58.8 1.3 reshape.127
  60.1 1.5 broadcast_multiply_fusion
  61.6 0.8 fusion.13
  62.4 0.1 convert.28
  62.5 0.9 slice_bitcast_fusion.2
  63.4 1.3 collective-permute-start.3
  64.7 1.3 collective-permute-start.4
  66.0 1.5 collective-permute-start.5
  67.5 1.6 %pad_maximum_fusion.1 = f32[512,4,128]{2,1,0:T(4,128)} fusion(f32[512,4,64]{2,1,0:T(4,128)S(1)} %get-tuple-element.16, f32[512,4,64]{2,1,0:T(4,128)S(1)} %get-tuple-element.15), kind=kLoop, calls=%fused_computation.13 | loop fusion | flops 262144 | bytes 2097152 | tf_op jit(solution)/shard_map/concatenate | solution.py:39
  69.1 8.3 %shard_map.77 = bf16[4096,512]{1,0:T(8,128)(2,1)} custom-call(bf16[512,4096]{1,0:T(8,128)(2,1)} %bitcast.57, bf16[512,512]{1,0:T(8,128)(2,1)} %copy-done.1), custom_call_target="tpu_custom_call" | custom-call | flops 2147483648 | bytes 8912896 | tf_op jit(solution)/shard_map/pallas_call | solution.py:344
  77.4 1.9 %fusion.1 = bf16[512,512]{1,0:T(8,128)(2,1)S(1)} fusion(f32[64,8,4,128]{3,2,1,0:T(4,128)} %bitcast.55, f32[512,512]{1,0:T(8,128)S(1)} %get-tuple-element.8, f32[64,8,4,128]{3,2,1,0:T(4,128)} %bitcast.54), kind=kLoop, calls=%fused_computation.4 | loop fusion | flops 786432 | bytes 3670016 | tf_op jit(solution)/shard_map/convert
  79.3 0.1 collective-permute-done.4
  79.3 1.4 collective-permute-done.5
  80.7 1.1 fusion.4
  81.9 0.9 slice_multiply_fusion.1
  82.8 0.1 fusion.14
  83.0 1.0 fusion.7
  84.0 0.9 pad_maximum_fusion.2.mg_ref
  84.9 7.8 %fusion = bf16[1,512,4096]{2,1,0:T(8,128)(2,1)} fusion(bf16[4096,768]{1,0:T(8,128)(2,1)} %param.7, bf16[512,128]{1,0:T(8,128)(2,1)S(1)} %slice.108, bf16[512,128]{1,0:T(8,128)(2,1)S(1)} %fusion.7, bf16[512,512]{1,0:T(8,128)(2,1)S(1)} %fusion.1), kind=kOutput, calls=%fused_computation.1 | convolution fusion | flops 3225681920 | bytes 11272192 | tf_op jit(solution)/shard_map/dot_general | solution.py:409
  92.7 56.1 %shard_map.78 = (f32[32,768]{1,0:T(8,128)}, f32[32,512]{1,0:T(8,128)}) custom-call(bf16[512,4096]{1,0:T(8,128)(2,1)} %bitcast.58, bf16[512,768]{1,0:T(8,128)(2,1)} %pad_maximum_fusion.2.mg_ref, bf16[32,2,64,512]{3,2,1,0:T(8,128)(2,1)} %bitcast.52), custom_call_target="tpu_custom_call" | custom-call | tf_op jit(solution)/shard_map/pallas_call | solution.py:226
  148.8 1.5 %copy.18 = f32[32,768]{1,0:T(8,128)} copy(f32[32,768]{1,0:T(8,128)} %get-tuple-element.32) | data formatting | bytes 196608
  150.4 1.5 copy.19
  (20 shorter events, 0.1 us)
Async XLA Ops:
  0.7 7.1 %copy-start.9 = (s32[1,512]{1,0:T(1,128)S(1)}, s32[1,512]{1,0:T(1,128)}, u32[]{:S(2)}) copy-start(s32[1,512]{1,0:T(1,128)} %param.9) | copy-start | bytes 6148
  8.0 0.7 copy-start.5
  9.9 21.2 %copy-start.7 = (f32[512,128]{1,0:T(8,128)}, f32[512,128]{1,0:T(8,128)S(1)}, u32[]{:S(2)}) copy-start(f32[512,128]{1,0:T(8,128)S(1)} %get-tuple-element.25) | copy-start | bytes 786436
  10.7 22.5 %collective-permute-start = (bf16[512,256]{1,0:T(8,128)(2,1)}, bf16[512,256]{1,0:T(8,128)(2,1)}, u32[]{:S(2)}, u32[]{:S(2)}) collective-permute-start(bf16[512,256]{1,0:T(8,128)(2,1)} %pad_maximum_fusion.4), channel_id=1, source_target_pairs={{0,2},{2,4},{4,6},{6,8},{8,10},{10,12},{12,14},{14,16},{16,18},{18... | collective-permute-start | bytes 786440 | tf_op jit(solution)/shard_map/ppermute | solution.py:19
  12.6 20.6 %collective-permute-start.1 = (bf16[512,256]{1,0:T(8,128)(2,1)}, bf16[512,256]{1,0:T(8,128)(2,1)}, u32[]{:S(2)}, u32[]{:S(2)}) collective-permute-start(bf16[512,256]{1,0:T(8,128)(2,1)} %pad_maximum_fusion.4), channel_id=1, source_target_pairs={{0,4},{2,6},{4,8},{6,10},{8,12},{10,14},{12,16},{14,18},{16,20},{1... | collective-permute-start | bytes 786440 | tf_op jit(solution)/shard_map/ppermute | solution.py:19
  16.8 16.5 %collective-permute-start.2 = (bf16[512,256]{1,0:T(8,128)(2,1)}, bf16[512,256]{1,0:T(8,128)(2,1)}, u32[]{:S(2)}, u32[]{:S(2)}) collective-permute-start(bf16[512,256]{1,0:T(8,128)(2,1)} %pad_maximum_fusion.4), channel_id=1, source_target_pairs={{0,6},{2,8},{4,10},{6,12},{8,14},{10,16},{12,18},{14,20},{16,22},{... | collective-permute-start | bytes 786440 | tf_op jit(solution)/shard_map/ppermute | solution.py:19
  23.5 2.2 %copy-start.4 = (bf16[1,512,4096]{2,1,0:T(8,128)(2,1)S(1)}, bf16[1,512,4096]{2,1,0:T(8,128)(2,1)}, u32[]{:S(2)}) copy-start(bf16[1,512,4096]{2,1,0:T(8,128)(2,1)} %param.6) | copy-start | bytes 12582916
  31.9 1.1 copy-start.3
  33.2 1.3 copy-start
  34.5 1.0 copy-start.2
  58.0 0.8 copy-start.1
  58.8 1.3 copy-start.8
  63.4 15.9 %collective-permute-start.3 = (bf16[512,256]{1,0:T(8,128)(2,1)}, bf16[512,256]{1,0:T(8,128)(2,1)S(1)}, u32[]{:S(2)}, u32[]{:S(2)}) collective-permute-start(bf16[512,256]{1,0:T(8,128)(2,1)} %get-tuple-element.17), channel_id=1, source_target_pairs={{2,0},{4,2},{6,4},{8,6},{10,8},{12,10},{14,12},{16,14},{18,16},{20... | collective-permute-start | bytes 786440 | tf_op jit(solution)/shard_map/ppermute | solution.py:19
  64.7 14.6 %collective-permute-start.4 = (bf16[512,256]{1,0:T(8,128)(2,1)}, bf16[512,256]{1,0:T(8,128)(2,1)}, u32[]{:S(2)}, u32[]{:S(2)}) collective-permute-start(bf16[512,256]{1,0:T(8,128)(2,1)} %get-tuple-element.19), channel_id=1, source_target_pairs={{4,0},{6,2},{8,4},{10,6},{12,8},{14,10},{16,12},{18,14},{20,16},{2... | collective-permute-start | bytes 786440 | tf_op jit(solution)/shard_map/ppermute | solution.py:19
  66.0 14.7 %collective-permute-start.5 = (bf16[512,256]{1,0:T(8,128)(2,1)}, bf16[512,256]{1,0:T(8,128)(2,1)}, u32[]{:S(2)}, u32[]{:S(2)}) collective-permute-start(bf16[512,256]{1,0:T(8,128)(2,1)} %get-tuple-element.18), channel_id=1, source_target_pairs={{6,0},{8,2},{10,4},{12,6},{14,8},{16,10},{18,12},{20,14},{22,16},{... | collective-permute-start | bytes 786440 | tf_op jit(solution)/shard_map/ppermute | solution.py:19
  77.4 4.5 %copy-start.6 = (f32[512,64]{1,0:T(8,128)S(1)}, f32[512,64]{1,0:T(8,128)}, u32[]{:S(2)}) copy-start(f32[512,64]{1,0:T(8,128)} %copy-done.5) | copy-start | bytes 393220

commit v3 on v2

--- a/solution.py
+++ b/solution.py
@@ -13,32 +13,12 @@
 rope_theta = 500000.0
 
 
-def from_behind(block, axis, distance):
-    devices = range(lax.axis_size(axis))
-    route = [(i - distance, i) for i in devices if i - distance in devices]
-    return lax.ppermute(block, axis, route)
-
-
 def rope_tables(offsets):
     half_width = HEAD // 2
     frequency = rope_theta ** (-2.0 * jnp.arange(half_width, dtype=jnp.float32) / HEAD)
     angles = offsets.astype(jnp.float32)[:, None] * frequency[None, :]
-    angles = jnp.concatenate([angles, angles], axis=1)
-    return (jnp.cos(angles), jnp.sin(angles))
-
-
-def rotate(vector, cosine_table, sine_table):
-    half_width = vector.shape[-1] // 2
-    rotated = jnp.concatenate([-vector[..., half_width:], vector[..., :half_width]], axis=-1)
-    return vector * cosine_table + rotated * sine_table
-
-
-def rotate_back(gradient, cosine_table, sine_table):
-    half_width = gradient.shape[-1] // 2
-    weighted = gradient * sine_table
-    return gradient * cosine_table + jnp.concatenate(
-        [weighted[..., half_width:], -weighted[..., :half_width]], axis=-1
-    )
+    cosine, sine = jnp.cos(angles), jnp.sin(angles)
+    return (jnp.concatenate([cosine, cosine], axis=1), jnp.concatenate([-sine, sine], axis=1))
 
 
 AXES = 4
@@ -265,17 +245,62 @@
     return lax.dot_general(a, b, dims, preferred_element_type=F32)
 
 
-def attention_kernel(first_ref, q_ref, g_ref, kv_ref, start_ref, att_ref, dq_ref, dkv_ref):
+def middle_kernel(
+    proj_ref, up_ref, w_ref, start_ref, cos_ref, sin_ref, merged_ref, term_ref,
+    kv_ref, g_ref, att_ref, dkv_ref, far_ref, back_ref, send_sem, recv_sem,
+):
     scale = HEAD**-0.5
     c = scale * LOG2E
+    width = HEADS * HEAD
+    seq = lax.axis_index("seq")
+    dp_index = lax.axis_index("dp")
+    count = lax.axis_size("seq")
+    first = seq * TOK
+
+    def peer(distance):
+        return (lax.rem(seq + distance + count, count), dp_index)
+
+    barrier = pltpu.get_barrier_semaphore()
+    for d in range(1, SPAN):
+        for distance in (d, -d):
+            pl.semaphore_signal(barrier, inc=1, device_id=peer(distance), device_id_type=MESH_ID)
+
+    def turn(v, rows):
+        return v * cos_ref[rows, :] + pltpu.roll(v, HEAD // 2, 1) * sin_ref[rows, :]
+
+    def turn_back(v, rows):
+        return v * cos_ref[rows, :] + pltpu.roll(v * sin_ref[rows, :], HEAD // 2, 1)
+
+    everything = slice(0, TOK)
+    kv_ref[0, :, :HEAD] = turn(proj_ref[:, width : width + HEAD], everything).astype(BF16)
+    kv_ref[0, :, HEAD:] = proj_ref[:, width + HEAD :].astype(BF16)
     dkv_ref[...] = jnp.zeros_like(dkv_ref)
-    first = first_ref[0]
+    pl.semaphore_wait(barrier, 2 * (SPAN - 1))
+
+    def copy(n, src, dst, distance):
+        return pltpu.make_async_remote_copy(
+            src_ref=src,
+            dst_ref=dst,
+            send_sem=send_sem.at[n],
+            recv_sem=recv_sem.at[n],
+            device_id=peer(distance),
+            device_id_type=MESH_ID,
+        )
+
+    ahead = [copy(d - 1, kv_ref.at[0], kv_ref.at[d], d) for d in range(1, SPAN)]
+    for item in ahead:
+        item.start()
+    for block in range(TOK // QROWS):
+        rows = slice(block * QROWS, (block + 1) * QROWS)
+        g_ref[rows, :] = mm(up_ref[rows, :], w_ref[...], NT).astype(BF16)
+    for item in ahead:
+        item.wait_recv()
 
     def head(h, _):
         cols = pl.ds(pl.multiple_of(h * HEAD, HEAD), HEAD)
         for block in range(TOK // QROWS):
             rows = slice(block * QROWS, (block + 1) * QROWS)
-            q = q_ref[rows, cols]
+            q = turn(proj_ref[rows, cols], rows).astype(BF16)
             g = g_ref[rows, cols]
             start = start_ref[rows, :]
             widths = [(block + 1) * QROWS] + [TOK] * (SPAN - 1)
@@ -310,110 +335,77 @@
                 dq = dq + mm(ds, kv_ref[d, :w, :HEAD], NN)
                 dkv_ref[d, :w, :HEAD] += mm(ds, q, TN)
                 dkv_ref[d, :w, HEAD:] += mm(rounded[d], g, TN)
-            dq_ref[rows, cols] = dq * scale
+            merged_ref[rows, cols] = turn_back(dq * scale, rows).astype(BF16)
         return 0
 
     lax.fori_loop(0, HEADS, head, 0)
-    for d in range(SPAN):
-        dkv_ref[d, :, :HEAD] = dkv_ref[d, :, :HEAD] * scale
-
-
-def attention(first, q, g, kv, start):
+    for d in range(1, SPAN):
+        far_ref[d - 1, :, :HEAD] = (dkv_ref[d, :, :HEAD] * scale).astype(BF16)
+        far_ref[d - 1, :, HEAD:] = dkv_ref[d, :, HEAD:].astype(BF16)
+    behind = [copy(SPAN - 2 + d, far_ref.at[d - 1], back_ref.at[d - 1], -d) for d in range(1, SPAN)]
+    for item in behind:
+        item.start()
+
+    def term(i, _):
+        cols = pl.ds(pl.multiple_of(i * TOK, TOK), TOK)
+        term_ref[cols, :] = mm(up_ref[:, cols], att_ref[...], TN).astype(BF16)
+        return 0
+
+    lax.fori_loop(0, up_ref.shape[1] // TOK, term, 0)
+    for item in behind:
+        item.wait_recv()
+    key = dkv_ref[0, :, :HEAD] * scale
+    value = dkv_ref[0, :, HEAD:]
+    for d in range(SPAN - 1):
+        key = key + back_ref[d, :, :HEAD].astype(F32)
+        value = value + back_ref[d, :, HEAD:].astype(F32)
+    merged_ref[:, width : width + HEAD] = turn_back(key, everything).astype(BF16)
+    merged_ref[:, width + HEAD :] = value.astype(BF16)
+    for item in ahead + behind:
+        item.wait_send()
+
+
+def middle(projected, upstream, w_out, start, cosine, sine):
     vmem = pl.BlockSpec(memory_space=pltpu.VMEM)
+    width = HEADS * HEAD
     return pl.pallas_call(
-        attention_kernel,
+        middle_kernel,
         out_shape=(
-            jax.ShapeDtypeStruct((TOK, HEADS * HEAD), BF16),
-            jax.ShapeDtypeStruct((TOK, HEADS * HEAD), F32),
-            jax.ShapeDtypeStruct((SPAN, TOK, 2 * HEAD), F32),
+            jax.ShapeDtypeStruct((TOK, width + 2 * HEAD), BF16),
+            jax.ShapeDtypeStruct((upstream.shape[1], width), BF16),
         ),
-        in_specs=[pl.BlockSpec(memory_space=pltpu.SMEM)] + [vmem] * 4,
-        out_specs=(vmem, vmem, vmem),
-        compiler_params=pltpu.CompilerParams(vmem_limit_bytes=48 * 1024 * 1024),
-    )(first, q, g, kv, start)
-
-
-def out_kernel(g_ref, att_ref, term_ref):
-    term_ref[...] = mm(g_ref[...], att_ref[...], TN).astype(BF16)
-
-
-def out_terms(upstream, attended):
-    rows, width = upstream.shape
-    cols = attended.shape[1]
-    step = 512
-    return pl.pallas_call(
-        out_kernel,
-        grid=(width // step,),
-        out_shape=jax.ShapeDtypeStruct((width, cols), BF16),
-        in_specs=[
-            pl.BlockSpec((rows, step), lambda i: (0, i)),
-            pl.BlockSpec((rows, cols), lambda i: (0, 0)),
+        in_specs=[vmem] * 6,
+        out_specs=(vmem, vmem),
+        scratch_shapes=[
+            pltpu.VMEM((SPAN, TOK, 2 * HEAD), BF16),
+            pltpu.VMEM((TOK, width), BF16),
+            pltpu.VMEM((TOK, width), BF16),
+            pltpu.VMEM((SPAN, TOK, 2 * HEAD), F32),
+            pltpu.VMEM((SPAN - 1, TOK, 2 * HEAD), BF16),
+            pltpu.VMEM((SPAN - 1, TOK, 2 * HEAD), BF16),
+            pltpu.SemaphoreType.DMA((2 * (SPAN - 1),)),
+            pltpu.SemaphoreType.DMA((2 * (SPAN - 1),)),
         ],
-        out_specs=pl.BlockSpec((step, cols), lambda i: (i, 0)),
-        cost_estimate=pl.CostEstimate(
-            flops=2 * rows * width * cols,
-            bytes_accessed=2 * (rows * width + rows * cols + width * cols),
-            transcendentals=0,
+        compiler_params=pltpu.CompilerParams(
+            collective_id=1, has_side_effects=True, vmem_limit_bytes=60 * 1024 * 1024
         ),
-    )(upstream, attended)
+    )(projected, upstream, w_out, start, cosine, sine)
 
 
 def per_device(inputs, cotangent, w_qkv, w_out, doc_start):
     tokens = inputs[0]
-    upstream = cotangent[0]
     query_start = doc_start[0]
     rows_here = tokens.shape[0]
-    scaling = HEAD ** (-0.5)
-    query_width = HEADS * HEAD
     device_index = lax.axis_index("seq")
     query_pos = device_index * rows_here + jnp.arange(rows_here, dtype=jnp.int32)
-    cosine_table, sine_table = rope_tables(query_pos - query_start)
-    projected = jnp.dot(tokens, w_qkv, preferred_element_type=jnp.float32)
-    queries = rotate(
-        projected[:, :query_width].reshape(rows_here, HEADS, HEAD),
-        cosine_table[:, None, :],
-        sine_table[:, None, :],
-    ).astype(jnp.bfloat16)
-    rotated_keys = rotate(projected[:, query_width : query_width + HEAD], cosine_table, sine_table)
-    key_value = jnp.concatenate([rotated_keys, projected[:, query_width + HEAD :]], axis=1).astype(
-        jnp.bfloat16
+    cosine, sine = rope_tables(query_pos - query_start)
+    projected = jnp.dot(tokens, w_qkv, preferred_element_type=F32)
+    merged_grad, out_term = middle(
+        projected, cotangent[0], w_out, query_start.reshape(rows_here, 1), cosine, sine
     )
-    attended_grad = (
-        lax.dot_general(
-            upstream, w_out, (((1,), (1,)), ((), ())), preferred_element_type=jnp.float32
-        )
-        .astype(jnp.bfloat16)
-        .reshape(rows_here, HEADS, HEAD)
-    )
-    received = [key_value]
-    for offset in range(1, SPAN):
-        received.append(from_behind(key_value, "seq", offset))
-    attended, query_grad, kv_terms = attention(
-        (device_index * rows_here).reshape(1),
-        queries.reshape(rows_here, query_width),
-        attended_grad.reshape(rows_here, query_width),
-        jnp.stack(received),
-        query_start.reshape(rows_here, 1),
-    )
-    query_grad = query_grad.reshape(rows_here, HEADS, HEAD)
-    kv_total = kv_terms[0]
-    for offset in range(1, SPAN):
-        kv_total = kv_total + from_behind(kv_terms[offset].astype(BF16), "seq", -offset).astype(F32)
-    query_pre = rotate_back(query_grad, cosine_table[:, None, :], sine_table[:, None, :]).reshape(
-        rows_here, query_width
-    )
-    key_pre = rotate_back(kv_total[:, :HEAD], cosine_table, sine_table)
-    merged_grad = jnp.concatenate([query_pre, key_pre, kv_total[:, HEAD:]], axis=1).astype(
-        jnp.bfloat16
-    )
-    input_grad = lax.dot_general(
-        merged_grad, w_qkv, (((1,), (1,)), ((), ())), preferred_element_type=jnp.float32
-    ).astype(jnp.bfloat16)[None]
-    flat_attended = attended.reshape(rows_here, query_width)
-    out_term = out_terms(upstream, flat_attended)
+    input_grad = mm(merged_grad, w_qkv, NT).astype(BF16)[None]
     qkv_grad, out_rows = reduce_terms(tokens, merged_grad, out_term)
-    out_grad = out_rows.T
-    return (input_grad, qkv_grad, out_grad)
+    return (input_grad, qkv_grad, out_rows.T)
 
 
 def solution(mesh):

time: 153 us -> 140 us (0.915)
  Pallas kernels: 86.9 us -> 117 us
  starting transfers between devices: 14.2 us -> 0 us
  other arithmetic: 15.8 us -> 2.7 us
  local copies, waits for them, and re-layouts: 12.4 us -> 2.83 us
  matrix products: 20.2 us -> 16.4 us
    pallas_call x2 -> x1, Pallas kernels: 30.8 us -> 65.5 us  [middle(): pl.pallas_call(middle_kernel, out_shape=(jax.ShapeDtypeStruct((TOK, width...]
    ppermute x6 -> x0, starting transfers between devices: 14.2 us -> none  [from_behind(): return lax.ppermute(block, axis, route)]
    unnamed x22 -> x8, local copies, waits for them, and re-layouts: 7.11 us -> 1.28 us
    another operation x5 -> x0, other arithmetic: 5.4 us -> none
    pallas_call x1, Pallas kernels: 56.1 us -> 51.5 us  [reduce_terms(): pl.pallas_call(reduce_kernel, out_shape=(jax.ShapeDtypeStruct((ROWS, 768)...]
    dot_general x3 -> x2, matrix products: 20.2 us -> 16.4 us  [the longest x1 8.61 us: per_device(): projected = jnp.dot(tokens, w_qkv, preferred_element_type=F32)]
    mul x3 -> x0, other arithmetic: 3.09 us -> none  [the longest x2 2.43 us: rotate_back(): weighted = gradient * sine_table]
    reshape x2 -> x0, local copies, waits for them, and re-layouts: 2.87 us -> none  [the longest x1 1.56 us: per_device(): projected[:, :query_width].reshape(rows_here, HEADS, HEAD)]
  transfers between devices with their start and end apart: 6 -> 0, of which waited for: 2 -> 0; matrix products, arithmetic and copies ran while one was open for 9% -> 0% of each run, Pallas kernels for 5% -> 0%
where the time goes in v3:
time: 140 us
  Pallas kernels  117 us (84%)
  matrix products  16.4 us (12%)
  local copies, waits for them, and re-layouts  2.83 us (2%)
  other arithmetic  2.7 us (2%)
    pallas_call x1, Pallas kernels, middle(): pl.pallas_call(middle_kernel, out_shape=(jax.ShapeDtypeStruct((TOK, width...  65.5 us
    pallas_call x1, Pallas kernels, reduce_terms(): pl.pallas_call(reduce_kernel, out_shape=(jax.ShapeDtypeStruct((ROWS, 768)...  51.5 us
    dot_general x1, matrix products, per_device(): projected = jnp.dot(tokens, w_qkv, preferred_element_type=F32)  8.61 us
    dot_general x1, matrix products, mm(): return lax.dot_general(a, b, dims, preferred_element_type=F32)  7.82 us

profile of v3, /device:TPU:0, one launch (start us, length us, event | category | flops | bytes accessed | tf_op | source)
XLA Modules:
  0.0 139.6 jit_solution(16317534630325953182)
XLA Ops:
  0.6 0.7 subtract_convert_fusion
  1.3 1.5 %copy.8.start_ref = s32[512,1]{1,0:T(8,128)} copy(s32[512,1]{0,1:T(1,128)} %bitcast.18) | data formatting | bytes 4096 | tf_op jit(solution)/shard_map/reshape;squeeze | solution.py:404
  2.9 1.0 fusion.1
  3.9 1.0 pad_maximum_fusion
  4.9 8.6 %fusion.2.proj_ref = f32[512,768]{1,0:T(8,128)} fusion(bf16[4096,768]{1,0:T(8,128)(2,1)} %param.7, bf16[1,512,4096]{2,1,0:T(8,128)(2,1)} %param.5), kind=kOutput, calls=%fused_computation.9 | convolution fusion | flops 3221225472 | bytes 12058624 | tf_op jit(solution)/shard_map/dot_general | solution.py:402
  13.5 65.5 %shard_map.76 = (bf16[512,768]{1,0:T(8,128)(2,1)}, bf16[4096,512]{1,0:T(8,128)(2,1)}) custom-call(f32[512,768]{1,0:T(8,128)} %fusion.2.proj_ref, bf16[512,4096]{1,0:T(8,128)(2,1)} %bitcast.15, bf16[512,4096]{1,0:T(8,128)(2,1)} %w_ref.1, s32[512,1]{1,0:T(8,128)} %copy.8.start_ref, f32[512,128]{1,0:T(8,128)} %get-tuple-element.14.cos_ref, ...), custom_call_target="tpu_custom_call" | custom-call | tf_op jit(solution)/shard_map/pallas_call | solution.py:371
  79.0 0.0 copy-start
  79.0 51.5 %shard_map.77 = (f32[32,768]{1,0:T(8,128)}, f32[32,512]{1,0:T(8,128)}) custom-call(bf16[512,4096]{1,0:T(8,128)(2,1)} %bitcast.13, bf16[512,768]{1,0:T(8,128)(2,1)} %get-tuple-element.7.mg_ref, bf16[32,2,64,512]{3,2,1,0:T(8,128)(2,1)} %bitcast.14), custom_call_target="tpu_custom_call" | custom-call | tf_op jit(solution)/shard_map/pallas_call | solution.py:206
  130.5 0.0 copy-done
  130.5 0.0 copy-start.1
  130.5 0.0 copy-start.2
  130.5 7.8 %fusion = bf16[1,512,4096]{2,1,0:T(8,128)(2,1)} fusion(bf16[512,768]{1,0:T(8,128)(2,1)S(1)} %copy-done, bf16[4096,768]{1,0:T(8,128)(2,1)} %param.7), kind=kOutput, calls=%fused_computation.1 | convolution fusion | flops 3223322624 | bytes 11272192 | tf_op jit(solution)/shard_map/dot_general | solution.py:245
  138.3 0.0 copy-done.1
  138.3 0.6 copy.11
  139.0 0.0 copy-done.2
  139.0 0.6 copy.12
  (1 shorter events, 0.0 us)
Async XLA Ops:
  79.0 51.5 %copy-start = (bf16[512,768]{1,0:T(8,128)(2,1)S(1)}, bf16[512,768]{1,0:T(8,128)(2,1)}, u32[]{:S(2)}) copy-start(bf16[512,768]{1,0:T(8,128)(2,1)} %get-tuple-element.7.mg_ref) | copy-start | bytes 2359300
  130.5 7.8 %copy-start.1 = (f32[32,768]{1,0:T(8,128)S(1)}, f32[32,768]{1,0:T(8,128)}, u32[]{:S(2)}) copy-start(f32[32,768]{1,0:T(8,128)} %get-tuple-element.20) | copy-start | bytes 294916
  130.5 8.5 %copy-start.2 = (f32[32,512]{1,0:T(8,128)S(1)}, f32[32,512]{1,0:T(8,128)}, u32[]{:S(2)}) copy-start(f32[32,512]{1,0:T(8,128)} %get-tuple-element.10) | copy-start | bytes 196612

commit v4 on v3

--- a/solution.py
+++ b/solution.py
@@ -287,14 +287,21 @@
             device_id_type=MESH_ID,
         )
 
-    ahead = [copy(d - 1, kv_ref.at[0], kv_ref.at[d], d) for d in range(1, SPAN)]
-    for item in ahead:
-        item.start()
+    core = lax.rem(seq, 2)
+    hop = copy(0, kv_ref.at[0], kv_ref.at[2], 2)
+    near = copy(1, kv_ref.at[2], kv_ref.at[3 - 2 * core], 1 - 2 * core)
+    onward = copy(2, kv_ref.at[2 * core], kv_ref.at[1 + 2 * core], 1)
+    ahead = [hop, near, onward]
+    hop.start()
     for block in range(TOK // QROWS):
         rows = slice(block * QROWS, (block + 1) * QROWS)
         g_ref[rows, :] = mm(up_ref[rows, :], w_ref[...], NT).astype(BF16)
-    for item in ahead:
-        item.wait_recv()
+        if block == 0:
+            hop.wait_recv()
+            near.start()
+            onward.start()
+    near.wait_recv()
+    onward.wait_recv()
 
     def head(h, _):
         cols = pl.ds(pl.multiple_of(h * HEAD, HEAD), HEAD)

time: 140 us -> 135 us (0.964)
  Pallas kernels: 117 us -> 112 us
    pallas_call x1, Pallas kernels: 65.5 us -> 61 us  [middle(): pl.pallas_call(middle_kernel, out_shape=(jax.ShapeDtypeStruct((TOK, width...]
where the time goes in v4:
time: 135 us
  Pallas kernels  112 us (83%)
  matrix products  16.4 us (12%)
  local copies, waits for them, and re-layouts  2.83 us (2%)
  other arithmetic  2.7 us (2%)
    pallas_call x1, Pallas kernels, middle(): pl.pallas_call(middle_kernel, out_shape=(jax.ShapeDtypeStruct((TOK, width...  61 us
    pallas_call x1, Pallas kernels, reduce_terms(): pl.pallas_call(reduce_kernel, out_shape=(jax.ShapeDtypeStruct((ROWS, 768)...  51.3 us
    dot_general x1, matrix products, per_device(): projected = jnp.dot(tokens, w_qkv, preferred_element_type=F32)  8.61 us
    dot_general x1, matrix products, mm(): return lax.dot_general(a, b, dims, preferred_element_type=F32)  7.82 us

profile of v4, /device:TPU:0, one launch (start us, length us, event | category | flops | bytes accessed | tf_op | source)
XLA Modules:
  0.0 135.0 jit_solution(7617500930411296844)
XLA Ops:
  0.6 0.7 subtract_convert_fusion
  1.3 1.5 %copy.8.start_ref = s32[512,1]{1,0:T(8,128)} copy(s32[512,1]{0,1:T(1,128)} %bitcast.18) | data formatting | bytes 4096 | tf_op jit(solution)/shard_map/reshape;squeeze | solution.py:411
  2.9 1.0 fusion.1
  3.9 1.0 pad_maximum_fusion
  4.9 8.6 %fusion.2.proj_ref = f32[512,768]{1,0:T(8,128)} fusion(bf16[4096,768]{1,0:T(8,128)(2,1)} %param.7, bf16[1,512,4096]{2,1,0:T(8,128)(2,1)} %param.5), kind=kOutput, calls=%fused_computation.9 | convolution fusion | flops 3221225472 | bytes 12058624 | tf_op jit(solution)/shard_map/dot_general | solution.py:409
  13.5 61.0 %shard_map.76 = (bf16[512,768]{1,0:T(8,128)(2,1)}, bf16[4096,512]{1,0:T(8,128)(2,1)}) custom-call(f32[512,768]{1,0:T(8,128)} %fusion.2.proj_ref, bf16[512,4096]{1,0:T(8,128)(2,1)} %bitcast.15, bf16[512,4096]{1,0:T(8,128)(2,1)} %w_ref.1, s32[512,1]{1,0:T(8,128)} %copy.8.start_ref, f32[512,128]{1,0:T(8,128)} %get-tuple-element.14.cos_ref, ...), custom_call_target="tpu_custom_call" | custom-call | tf_op jit(solution)/shard_map/pallas_call | solution.py:378
  74.5 0.0 copy-start
  74.5 51.3 %shard_map.77 = (f32[32,768]{1,0:T(8,128)}, f32[32,512]{1,0:T(8,128)}) custom-call(bf16[512,4096]{1,0:T(8,128)(2,1)} %bitcast.13, bf16[512,768]{1,0:T(8,128)(2,1)} %get-tuple-element.7.mg_ref, bf16[32,2,64,512]{3,2,1,0:T(8,128)(2,1)} %bitcast.14), custom_call_target="tpu_custom_call" | custom-call | tf_op jit(solution)/shard_map/pallas_call | solution.py:206
  125.9 0.0 copy-done
  125.9 0.0 copy-start.1
  125.9 0.0 copy-start.2
  125.9 7.8 %fusion = bf16[1,512,4096]{2,1,0:T(8,128)(2,1)} fusion(bf16[512,768]{1,0:T(8,128)(2,1)S(1)} %copy-done, bf16[4096,768]{1,0:T(8,128)(2,1)} %param.7), kind=kOutput, calls=%fused_computation.1 | convolution fusion | flops 3223322624 | bytes 11272192 | tf_op jit(solution)/shard_map/dot_general | solution.py:245
  133.7 0.0 copy-done.1
  133.7 0.6 copy.11
  134.4 0.0 copy-done.2
  134.4 0.6 copy.12
  (1 shorter events, 0.0 us)
Async XLA Ops:
  74.5 51.4 %copy-start = (bf16[512,768]{1,0:T(8,128)(2,1)S(1)}, bf16[512,768]{1,0:T(8,128)(2,1)}, u32[]{:S(2)}) copy-start(bf16[512,768]{1,0:T(8,128)(2,1)} %get-tuple-element.7.mg_ref) | copy-start | bytes 2359300
  125.9 7.8 %copy-start.1 = (f32[32,768]{1,0:T(8,128)S(1)}, f32[32,768]{1,0:T(8,128)}, u32[]{:S(2)}) copy-start(f32[32,768]{1,0:T(8,128)} %get-tuple-element.20) | copy-start | bytes 294916
  125.9 8.5 %copy-start.2 = (f32[32,512]{1,0:T(8,128)S(1)}, f32[32,512]{1,0:T(8,128)}, u32[]{:S(2)}) copy-start(f32[32,512]{1,0:T(8,128)} %get-tuple-element.10) | copy-start | bytes 196612
